TPU v7x, 256 devices: a whole 4x4x8 slice. The times are simulated.
256 devices in a mesh: owner: 64 (over z, x, core), col: 4 (over y).
Axes of the slice: x: 4, y: 4, z: 8, core: 2. Of those that a mesh axis runs over, the one named last changes fastest.
Arguments:
- momentum: float32 [128, 512, 2048], P(None, 'owner', 'col'), may hold values from -7200 to 7200
- hidden_acts: bfloat16 [32768, 512], P('owner'), may hold values from -6 to 6
- output_grads: bfloat16 [32768, 2048], P('owner', 'col'), may hold values from -6 to 6
- routing: int32 [32768], P('owner'), may hold values from 0 to 1
- assignment: int32 [128], replicated, may hold values from 0 to 127, each once
Outputs:
- new_momentum: float32 [128, 512, 2048], P(None, 'owner', 'col')
- update: float32 [128, 512, 2048], P('owner', None, 'col')
Inputs may be any that keep to these rules, and one draw needn't show every extreme that they name: `routing`: the row's expert as a local slot of the owner group that holds the row. `assignment`: a permutation: each expert is held in exactly one slot.
All inputs are finite; a program needn't handle non-finite values.
Results may differ from a plain program's by a relative error of at most 0.0065.
Values may be sent and summed in bfloat16 or wider, within the bound.
A program may use at most 64 MiB of HBM per device.

v0:
```python
import jax
import jax.numpy as jnp
from jax import lax
from jax.sharding import Mesh
from jax.sharding import PartitionSpec as P

D = 2048
FFE = 512
EXP_DEV = 2
NS_ITERS = 2
OWNER = ("owner_0", "owner_1", "owner_2")


decay_rate = 0.95
epsilon = 1e-07
linear_weight = 3.4445
cubic_weight = -4.775
quintic_weight = 2.0315


def from_everyone(array, axis):
    copies = jnp.broadcast_to(array, (lax.axis_size(axis), *array.shape))
    return lax.all_to_all(copies, axis, split_axis=0, concat_axis=0, tiled=True)


def taken_together(array, axis):
    return from_everyone(array, axis).sum(axis=0)


def split_up(array, dim, size):
    shape = array.shape
    parts = array.reshape(*shape[:dim], size, shape[dim] // size, *shape[dim + 1 :])
    return jnp.moveaxis(parts, dim, 0)


def laid_out(parts, dim):
    shape = list(parts.shape[1:])
    shape[dim] *= parts.shape[0]
    return jnp.moveaxis(parts, 0, dim).reshape(shape)


def turned_blocks(parts, axes, sequence):
    shape = [lax.axis_size(a) for a in axes]
    parts = parts.reshape(*shape, *parts.shape[1:])
    for k in sequence:
        parts = lax.all_to_all(parts, axes[k], split_axis=k, concat_axis=k, tiled=True)
    return parts.reshape(-1, *parts.shape[len(axes) :])


def core_and_chips(array, groups, sequence, split_dim, concat_dim):
    size = lax.axis_size(groups[0]) * lax.axis_size(groups[1])
    parts = split_up(array, split_dim, size)
    return laid_out(turned_blocks(parts, groups, sequence), concat_dim)


def newton_turn(iterate, gram_matrix):
    square = jnp.einsum(
        "jfg,jgh->jfh", gram_matrix, gram_matrix, preferred_element_type=jnp.float32
    )
    polynomial = (cubic_weight * gram_matrix.astype(jnp.float32) + quintic_weight * square).astype(
        jnp.bfloat16
    )
    product = jnp.einsum("jfg,jgd->jfd", polynomial, iterate, preferred_element_type=jnp.float32)
    return (linear_weight * iterate.astype(jnp.float32) + product).astype(jnp.bfloat16)


def body(momentum, hidden_acts, output_grads, routing, assignment):
    scaling = 0.2 * float(max(FFE, D)) ** 0.5
    columns = output_grads.shape[1]
    ordered = jnp.take(momentum, assignment, axis=0)
    received = lax.all_to_all(ordered, OWNER, split_axis=0, concat_axis=1, tiled=True)
    slot_ids = jnp.arange(EXP_DEV, dtype=jnp.int32)
    selected = routing[:, None, None] == slot_ids[None, :, None]
    masked = jnp.where(selected, output_grads[:, None, :], jnp.zeros((), jnp.bfloat16))
    gradient = jnp.einsum("rf,rjd->jfd", hidden_acts, masked, preferred_element_type=jnp.float32)
    updated = decay_rate * received + gradient
    squares = taken_together(jnp.sum(updated * updated, axis=(1, 2)), "col")
    iterate = (updated / (jnp.sqrt(squares)[:, None, None] + epsilon)).astype(jnp.bfloat16)
    complete = lax.all_gather(iterate, "col", axis=2, tiled=True)
    for turn_index in range(NS_ITERS):
        gram_matrix = jnp.einsum(
            "jfd,jgd->jfg", complete, complete, preferred_element_type=jnp.float32
        ).astype(jnp.bfloat16)
        complete = newton_turn(complete, gram_matrix)
    result_cols = lax.dynamic_slice_in_dim(complete, lax.axis_index("col") * columns, columns, 2)
    update = scaling * result_cols.astype(jnp.float32)
    returned = core_and_chips(
        updated.astype(jnp.bfloat16), (("owner_0", "owner_1"), "owner_2"), (1, 0), 1, 0
    ).astype(updated.dtype)
    new_momentum = jnp.zeros_like(momentum).at[assignment].set(returned)
    return (new_momentum, update)


def solution(mesh):
    torus = Mesh(
        mesh.devices.reshape(8, 4, 2, mesh.shape["col"]), ("owner_0", "owner_1", "owner_2", "col")
    )
    return jax.shard_map(
        body,
        mesh=torus,
        in_specs=(P(None, OWNER, "col"), P(OWNER, None), P(OWNER, "col"), P(OWNER), P()),
        out_specs=(P(None, OWNER, "col"), P(OWNER, None, "col")),
        check_vma=False,
    )
```

profile of v0, /device:TPU:8, one launch (start us, length us, event | category | flops | bytes accessed | tf_op | source)
XLA Modules:
  0.0 191.5 jit_solution(2016149358250970594)
XLA Ops:
  7.2 0.0 copy-start
  7.2 0.8 compare_select_fusion
  8.0 0.7 compare_and_fusion
  8.7 0.1 copy-done
  8.8 2.1 %gather_fusion = f32[128,8,512]{2,1,0:T(8,128)} fusion(f32[128,8,512]{2,1,0:T(8,128)S(1)} %copy-done, s32[1024]{0:T(1024)S(1)} %pad_clamp_fusion), kind=kCustom, calls=%fused_computation | custom fusion | bytes 4194816 | tf_op jit(solution)/shard_map/jit(_take)/gather | solution.py:70
  10.9 3.1 %broadcast_select_fusion = f32[128,8,512]{2,1,0:T(8,128)} fusion(f32[128,8,512]{2,1,0:T(8,128)} %gather_fusion, pred[128]{0:T(512)(128)(4,1)S(1)} %compare_and_fusion), kind=kLoop, calls=%fused_computation.16 | loop fusion | flops 524288 | bytes 4194432 | tf_op jit(solution)/shard_map/jit(_take)/select_n | solution.py:70
  14.0 0.0 copy-start.1
  14.0 12.3 %all-to-all-start = ((f32[128,8,512]{2,1,0:T(8,128)}), f32[128,8,512]{2,1,0:T(8,128)}, u32[]{:S(2)}, u32[]{:S(2)}) async-start(f32[128,8,512]{2,1,0:T(8,128)} %broadcast_select_fusion), calls=%async_computation | async-start | bytes 4194304 | tf_op jit(solution)/shard_map/all_to_all | solution.py:71
  26.4 0.0 all-gather.2.cloned.1.call-start
  26.4 0.0 copy-done.1
  26.4 0.0 copy-start.2
  26.4 51.1 %all-to-all-done = f32[128,8,512]{2,1,0:T(8,128)} async-done(((f32[128,8,512]{2,1,0:T(8,128)}), f32[128,8,512]{2,1,0:T(8,128)}, u32[]{:S(2)}, u32[]{:S(2)}) %all-to-all-start) | async-done | bytes 2097184 | tf_op jit(solution)/shard_map/all_to_all | solution.py:71
  77.5 1.9 broadcast_multiply_fusion
  79.4 0.0 copy-done.2
  79.4 0.0 copy-done.3
  79.4 2.2 %multiply_reduce_fusion = (f32[2]{0:T(128)S(1)}, f32[2,512,512]{2,1,0:T(8,128)}) fusion(bf16[512,512]{1,0:T(8,128)(2,1)S(1)} %copy-done.2, pred[512,2]{0,1:T(4,128)(4,1)S(1)} %iota_compare_fusion, bf16[512,512]{1,0:T(8,128)(2,1)S(1)} %copy-done.3, f32[64,2,8,512]{3,2,1,0:T(8,128)S(1)} %bitcast.31), kind=kOutput, calls=%fused_computation.10 | convolution fusion | flops 538968064 | bytes 5243912 | tf_op jit(solution)/shard_map/rf,rjd->jfd/dot_general | solution.py:75
  81.7 8.5 %all_to_all.25 = f32[4,1,2]{2,1,0:T(1,128)S(1)} all-to-all(f32[4,1,2]{2,1,0:T(1,128)S(1)} %broadcast_in_dim.50), channel_id=1, replica_groups=mesh['owner_0'=8,'owner_1'=4,'owner_2'=2,'col'=4] {'col'}, dimensions={0} | all-to-all | bytes 64 | tf_op jit(solution)/shard_map/all_to_all | solution.py:23
  90.2 3.6 %divide_convert_fusion = (bf16[2,512,512]{2,1,0:T(8,128)(2,1)}, bf16[2,512,512]{2,1,0:T(8,128)(2,1)S(1)}) fusion(f32[2,512,512]{2,1,0:T(8,128)} %get-tuple-element.5, f32[2]{0:T(128)S(1)} %sqrt_add_fusion), kind=kLoop, calls=%fused_computation.9 | loop fusion | flops 1572864 | bytes 4194312 | tf_op jit(solution)/shard_map/convert_element_type | solution.py:78
  93.9 0.0 all-gather.2.cloned.1.call-update
  93.9 0.2 copy.28
  94.1 4.6 %all_to_all.26 = bf16[32,2,2,8,512]{4,3,2,0,1:T(8,128)(2,1)S(1)} all-to-all(bf16[32,2,2,8,512]{4,3,2,0,1:T(8,128)(2,1)S(1)} %copy.28), channel_id=1, replica_groups=mesh['owner_0'=8,'owner_1'=4,'owner_2'=2,'col'=4] {'owner_2'}, dimensions={1} | all-to-all | bytes 2097152 | tf_op jit(solution)/shard_map/all_to_all | solution.py:46
  98.6 1.1 copy.29
  99.7 4.9 %all-to-all-start.2 = ((bf16[32,2,2,8,512]{4,3,2,1,0:T(8,128)(2,1)}), bf16[32,2,2,8,512]{4,3,2,1,0:T(8,128)(2,1)S(1)}, u32[]{:S(2)}, u32[]{:S(2)}) async-start(bf16[32,2,2,8,512]{4,3,2,1,0:T(8,128)(2,1)} %copy.29), calls=%async_computation.2 | async-start | bytes 2097152 | tf_op jit(solution)/shard_map/all_to_all | solution.py:46
  104.6 28.2 %all-to-all-done.2 = bf16[32,2,2,8,512]{4,3,2,1,0:T(8,128)(2,1)S(1)} async-done(((bf16[32,2,2,8,512]{4,3,2,1,0:T(8,128)(2,1)}), bf16[32,2,2,8,512]{4,3,2,1,0:T(8,128)(2,1)S(1)}, u32[]{:S(2)}, u32[]{:S(2)}) %all-to-all-start.2) | async-done | bytes 1048608 | tf_op jit(solution)/shard_map/all_to_all | solution.py:46
  132.8 1.7 bitcast_convert_fusion
  134.5 1.6 broadcast_in_dim.43
  136.0 17.6 %scatter_fusion = f32[128,8,512]{2,1,0:T(8,128)} fusion(f32[128,8,512]{2,1,0:T(8,128)} %broadcast_in_dim.43, s32[128]{0:T(128)S(1)} %compare_select_fusion, f32[128,8,512]{2,1,0:T(8,128)} %bitcast_convert_fusion), kind=kCustom, calls=%fused_computation.1 | custom fusion | bytes 6291968 | tf_op jit(solution)/shard_map/scatter | solution.py:90
  153.7 5.8 %convolution_convert_fusion.1 = bf16[2,512,512]{2,1,0:T(8,128)(2,1)S(1)} fusion(bf16[2,512,2048]{2,1,0:T(8,128)(2,1)} %all-gather.2.cloned.1.call-done), kind=kOutput, calls=%fused_computation.12 | convolution fusion | flops 2148007936 | bytes 5242880 | tf_op jit(solution)/shard_map/jfd,jgd->jfg/dot_general | solution.py:81
  159.5 7.4 %add_convert_fusion = bf16[2,512,2048]{2,1,0:T(8,128)(2,1)} fusion(bf16[2,512,2048]{2,1,0:T(8,128)(2,1)} %all-gather.2.cloned.1.call-done, bf16[2,512,512]{2,1,0:T(8,128)(2,1)S(1)} %convolution_convert_fusion.1), kind=kOutput, calls=%fused_computation.2 | convolution fusion | flops 2695364608 | bytes 9437184 | tf_op jit(solution)/shard_map/jfg,jgd->jfd/dot_general | solution.py:63
  166.9 5.8 %convolution_convert_fusion = bf16[2,512,512]{2,1,0:T(8,128)(2,1)S(1)} fusion(bf16[2,512,2048]{2,1,0:T(8,128)(2,1)} %add_convert_fusion), kind=kOutput, calls=%fused_computation.11 | convolution fusion | flops 2148007936 | bytes 5242880 | tf_op jit(solution)/shard_map/jfd,jgd->jfg/dot_general | solution.py:81
  172.7 8.3 %fusion.3 = f32[2,512,2048]{2,1,0:T(8,128)} fusion(bf16[2,512,2048]{2,1,0:T(8,128)(2,1)} %add_convert_fusion, bf16[2,512,512]{2,1,0:T(8,128)(2,1)S(1)} %convolution_convert_fusion), kind=kOutput, calls=%fused_computation.18 | convolution fusion | flops 2686976000 | bytes 13631488 | tf_op jit(solution)/shard_map/jfg,jgd->jfd/dot_general | solution.py:63
  181.0 3.6 %convert_multiply_fusion = f32[2,512,512]{2,1,0:T(8,128)} fusion(f32[2,512,2048]{2,1,0:T(8,128)} %fusion.3, s32[]{:T(128)S(6)} %select_n.20, bf16[2,512,2048]{2,1,0:T(8,128)(2,1)} %add_convert_fusion), kind=kLoop, calls=%fused_computation.6 | loop fusion | flops 3145728 | bytes 5242884 | tf_op jit(solution)/shard_map/mul | solution.py:86
  (7 shorter events, 0.1 us)
Async XLA Ops:
  7.2 1.6 copy-start
  14.0 12.4 %copy-start.1 = (s32[512]{0:T(512)S(1)}, s32[512]{0:T(512)}, u32[]{:S(2)}) copy-start(s32[512]{0:T(512)} %param.8) | copy-start | bytes 6148
  14.0 63.5 %all-to-all-start = ((f32[128,8,512]{2,1,0:T(8,128)}), f32[128,8,512]{2,1,0:T(8,128)}, u32[]{:S(2)}, u32[]{:S(2)}) async-start(f32[128,8,512]{2,1,0:T(8,128)} %broadcast_select_fusion), calls=%async_computation | async-start | bytes 4194304 | tf_op jit(solution)/shard_map/all_to_all | solution.py:71
  26.4 127.3 %all-gather.2.cloned.1.call-start = ((), (), s32[]{:S(2)}) async-start(), calls=%async_computation.4 | async-start | bytes 5242880 | tf_op jit(solution)/shard_map/all_gather | solution.py:79
  26.4 53.0 %copy-start.2 = (bf16[512,512]{1,0:T(8,128)(2,1)S(1)}, bf16[512,512]{1,0:T(8,128)(2,1)}, u32[]{:S(2)}) copy-start(bf16[512,512]{1,0:T(8,128)(2,1)} %param.6) | copy-start | bytes 1572868
  77.5 1.9 copy-start.3
  99.7 33.1 %all-to-all-start.2 = ((bf16[32,2,2,8,512]{4,3,2,1,0:T(8,128)(2,1)}), bf16[32,2,2,8,512]{4,3,2,1,0:T(8,128)(2,1)S(1)}, u32[]{:S(2)}, u32[]{:S(2)}) async-start(bf16[32,2,2,8,512]{4,3,2,1,0:T(8,128)(2,1)} %copy.29), calls=%async_computation.2 | async-start | bytes 2097152 | tf_op jit(solution)/shard_map/all_to_all | solution.py:46
Sparse Core Ops, SparseCore 0:
  94.0 45.3 all-gather.1
where the time goes:
time: 193 us; the launch traced here: 191 us
  waiting for transfers between devices  79.3 us (41%)
  matrix products  29.6 us (15%)
  local copies, waits for them, and re-layouts  22.7 us (12%)
  starting transfers between devices  17.3 us (9%)
  other arithmetic  15.4 us (8%)
  between operations  14.1 us (7%)
  blocking collectives  13.1 us (7%)
    all_to_all x1, waiting for transfers between devices, body(): lax.all_to_all(ordered, OWNER, split_axis=0, concat_axis=1, tiled=True)  51.1 us
    all_to_all x1, waiting for transfers between devices, turned_blocks(): lax.all_to_all(parts, axes[k], split_axis=k, concat_axis=k, tiled=True)  28.2 us
    scatter x1, local copies, waits for them, and re-layouts, body(): new_momentum = jnp.zeros_like(momentum).at[assignment].set(returned)  17.6 us
    dot_general x2, matrix products, newton_turn(): jnp.einsum('jfg,jgd->jfd', polynomial, iterate, preferred_element_type=jn...  15.7 us
    all_to_all x1, starting transfers between devices, body(): lax.all_to_all(ordered, OWNER, split_axis=0, concat_axis=1, tiled=True)  12.3 us
    dot_general x2, matrix products, body(): jnp.einsum('jfd,jgd->jfg', complete, complete, preferred_element_type=jnp...  11.6 us
    all_to_all x1, blocking collectives, from_everyone(): return lax.all_to_all(copies, axis, split_axis=0, concat_axis=0, tiled=True)  8.52 us
    all_to_all x1, starting transfers between devices, turned_blocks(): lax.all_to_all(parts, axes[k], split_axis=k, concat_axis=k, tiled=True)  4.89 us
  transfers between devices with their start and end apart: 3, of which 2 were waited for; matrix products, arithmetic and copies ran while one was open for 12% of the time, Pallas kernels for 0%

commit v1 on v0

v1 whole, which is shorter than its diff:
```python
import jax
import jax.numpy as jnp
from jax import lax
from jax.sharding import Mesh
from jax.sharding import PartitionSpec as P

D = 2048
FFE = 512
EXP_DEV = 2
OWNER = ("owner_0", "owner_1", "owner_2")

decay_rate = 0.95
epsilon = 1e-07
linear_weight = 3.4445
cubic_weight = -4.775
quintic_weight = 2.0315


def mm(a, b):
    return jnp.einsum(
        "jab,jbc->jac",
        a.astype(jnp.bfloat16),
        b.astype(jnp.bfloat16),
        preferred_element_type=jnp.float32,
    )


def body(momentum, hidden_acts, output_grads, routing, assignment):
    scaling = 0.2 * float(max(FFE, D)) ** 0.5
    n_col = lax.axis_size("col")
    order = assignment[:, None] == jnp.arange(assignment.shape[0], dtype=jnp.int32)[None, :]
    place = jnp.sum(
        jnp.where(order, jnp.arange(assignment.shape[0], dtype=jnp.int32)[:, None], 0), axis=0
    )
    ordered = momentum.at[assignment].get(mode="promise_in_bounds").astype(jnp.bfloat16)
    received = lax.all_to_all(ordered, OWNER, split_axis=0, concat_axis=1, tiled=True)
    slot_ids = jnp.arange(EXP_DEV, dtype=jnp.int32)
    selected = routing[:, None, None] == slot_ids[None, :, None]
    masked = jnp.where(selected, output_grads[:, None, :], jnp.zeros((), jnp.bfloat16))
    gradient = jnp.einsum("rf,rjd->jfd", hidden_acts, masked, preferred_element_type=jnp.float32)
    sent, _ = lax.optimization_barrier((gradient.astype(jnp.bfloat16), received))
    returned = lax.all_to_all(sent, OWNER, split_axis=1, concat_axis=0, tiled=True)
    updated = decay_rate * received.astype(jnp.float32) + gradient
    ub = updated.astype(jnp.bfloat16)
    partial = jnp.einsum("jfd,jgd->jfg", ub, ub, preferred_element_type=jnp.float32)
    pieces = lax.all_to_all(
        partial.astype(jnp.bfloat16).reshape(EXP_DEV, n_col, FFE // n_col, FFE),
        "col",
        split_axis=1,
        concat_axis=1,
        tiled=True,
    )
    piece = jnp.sum(pieces.astype(jnp.float32), axis=1).astype(jnp.bfloat16)
    full = lax.all_to_all(
        jnp.broadcast_to(piece[:, None], (EXP_DEV, n_col, FFE // n_col, FFE)),
        "col",
        split_axis=1,
        concat_axis=1,
        tiled=True,
    ).reshape(EXP_DEV, FFE, FFE)
    raw = full.astype(jnp.float32)
    eye = jnp.eye(FFE, dtype=jnp.bool_)[None]
    squares = jnp.sum(jnp.where(eye, raw, 0.0), axis=(1, 2), keepdims=True)
    inverse = 1.0 / (jnp.sqrt(squares) + epsilon)
    g1 = ((raw * inverse) * inverse).astype(jnp.bfloat16)
    p1 = (cubic_weight * g1.astype(jnp.float32) + quintic_weight * mm(g1, g1)).astype(jnp.bfloat16)
    t = mm(g1, p1)
    g2 = (
        linear_weight**2 * g1.astype(jnp.float32) + 2.0 * linear_weight * t + mm(p1, t)
    ).astype(jnp.bfloat16)
    p2 = (cubic_weight * g2.astype(jnp.float32) + quintic_weight * mm(g2, g2)).astype(jnp.bfloat16)
    rest = linear_weight * (p1.astype(jnp.float32) + p2.astype(jnp.float32)) + mm(p2, p1)
    update = (scaling * inverse) * (linear_weight**2 * updated + mm(rest, ub))
    back = returned.at[place].get(mode="promise_in_bounds")
    new_momentum = decay_rate * momentum + back.astype(jnp.float32)
    return (new_momentum, update)


def solution(mesh):
    torus = Mesh(
        mesh.devices.reshape(8, 4, 2, mesh.shape["col"]), ("owner_0", "owner_1", "owner_2", "col")
    )
    return jax.shard_map(
        body,
        mesh=torus,
        in_specs=(P(None, OWNER, "col"), P(OWNER, None), P(OWNER, "col"), P(OWNER), P()),
        out_specs=(P(None, OWNER, "col"), P(OWNER, None, "col")),
        check_vma=False,
    )
```

time: 193 us -> 135 us (0.70)
  waiting for transfers between devices: 79.3 us -> 44.3 us
  between operations: 14.1 us -> 0.81 us
  matrix products: 29.6 us -> 18.3 us
  other arithmetic: 15.4 us -> 4.65 us
  starting transfers between devices: 17.3 us -> 24.6 us
  blocking collectives: 13.1 us -> 17.9 us
    all_to_all x1, waiting for transfers between devices: 51.1 us -> 26.8 us  [body(): lax.all_to_all(ordered, OWNER, split_axis=0, concat_axis=1, tiled=True)]
    scatter x1 -> x0, local copies, waits for them, and re-layouts: 17.6 us -> none  [body(): new_momentum = jnp.zeros_like(momentum).at[assignment].set(returned)]
    dot_general x4 -> x6, matrix products: 27.3 us -> 16.6 us  [the longest x5 14.2 us: mm(): jnp.einsum('jab,jbc->jac', a.astype(jnp.bfloat16), b.astype(jnp.bfloat16)...]
    all_to_all x1 -> x2, waiting for transfers between devices: 28.2 us -> 17.5 us  [the longest x1 9.61 us: body(): lax.all_to_all(jnp.broadcast_to(piece[:, None], (EXP_DEV, n_col, FFE // n...]
    all_to_all x1 -> x2, starting transfers between devices: 4.89 us -> 12.3 us  [the longest x1 7.32 us: body(): lax.all_to_all(sent, OWNER, split_axis=1, concat_axis=0, tiled=True)]
    all_to_all x1 -> x4, local copies, waits for them, and re-layouts: 1.06 us -> 7.12 us  [the longest x2 4.6 us: body(): lax.all_to_all(ordered, OWNER, split_axis=0, concat_axis=1, tiled=True)]
    mul x2 -> x1, other arithmetic: 5.47 us -> 0.01 us  [body(): update = scaling * inverse * (linear_weight ** 2 * updated + mm(rest, ub))]
    convert_element_type x2 -> x0, other arithmetic: 5.31 us -> none  [the longest x1 3.63 us: body(): (updated / (jnp.sqrt(squares)[:, None, None] + epsilon)).astype(jnp.bfloa...]
  transfers between devices with their start and end apart: 3 -> 3, of which waited for: 2 -> 3; matrix products, arithmetic and copies ran while one was open for 12% -> 19% of each run, Pallas kernels for 0% -> 0%
where the time goes in v1:
time: 135 us; the launch traced here: 133 us
  waiting for transfers between devices  44.3 us (33%)
  starting transfers between devices  24.6 us (18%)
  local copies, waits for them, and re-layouts  22.8 us (17%)
  matrix products  18.3 us (14%)
  blocking collectives  17.9 us (13%)
  other arithmetic  4.65 us (3%)
    all_to_all x1, waiting for transfers between devices, body(): lax.all_to_all(ordered, OWNER, split_axis=0, concat_axis=1, tiled=True)  26.8 us
    all_to_all x1, blocking collectives, body(): lax.all_to_all(partial.astype(jnp.bfloat16).reshape(EXP_DEV, n_col, FFE /...  17.9 us
    dot_general x5, matrix products, mm(): jnp.einsum('jab,jbc->jac', a.astype(jnp.bfloat16), b.astype(jnp.bfloat16)...  14.2 us
    all_to_all x1, starting transfers between devices, body(): lax.all_to_all(ordered, OWNER, split_axis=0, concat_axis=1, tiled=True)  12.3 us
    all_to_all x1, waiting for transfers between devices, body(): lax.all_to_all(jnp.broadcast_to(piece[:, None], (EXP_DEV, n_col, FFE // n...  9.61 us
    all_to_all x1, waiting for transfers between devices, body(): lax.all_to_all(sent, OWNER, split_axis=1, concat_axis=0, tiled=True)  7.91 us
    all_to_all x1, starting transfers between devices, body(): lax.all_to_all(sent, OWNER, split_axis=1, concat_axis=0, tiled=True)  7.32 us
    all_to_all x1, starting transfers between devices, body(): lax.all_to_all(jnp.broadcast_to(piece[:, None], (EXP_DEV, n_col, FFE // n...  4.94 us
  transfers between devices with their start and end apart: 3, of which 3 were waited for; matrix products, arithmetic and copies ran while one was open for 19% of the time, Pallas kernels for 0%

profile of v1, /device:TPU:8, one launch (start us, length us, event | category | flops | bytes accessed | tf_op | source)
XLA Modules:
  0.0 133.3 jit_solution(5423864777520302218)
XLA Ops:
  0.6 0.7 compare_select_fusion.1
  1.4 3.4 %gather_fusion = bf16[128,8,512]{2,1,0:T(8,128)(2,1)} fusion(f32[128,8,512]{2,1,0:T(8,128)} %param.5, s32[1024]{0:T(1024)S(1)} %pad_clamp_fusion.1), kind=kCustom, calls=%fused_computation | custom fusion | bytes 2097664 | tf_op jit(solution)/shard_map/gather | solution.py:35
  4.7 12.3 %all-to-all-start = ((bf16[128,8,512]{2,1,0:T(8,128)(2,1)}), bf16[128,8,512]{2,1,0:T(8,128)(2,1)}, u32[]{:S(2)}, u32[]{:S(2)}) async-start(bf16[128,8,512]{2,1,0:T(8,128)(2,1)} %gather_fusion), calls=%async_computation | async-start | bytes 2097152 | tf_op jit(solution)/shard_map/all_to_all | solution.py:36
  17.1 0.2 copy.102
  17.3 1.7 %bitcast_convert_fusion = (bf16[2,512,512]{1,2,0:T(8,128)(2,1)}, f32[2,512,512]{2,1,0:T(8,128)S(1)}) fusion(bf16[512,512]{1,0:T(8,128)(2,1)S(1)} %copy-done, pred[512,2]{0,1:T(4,128)(4,1)S(1)} %iota_compare_fusion.2, bf16[512,512]{0,1:T(8,128)(2,1)S(1)} %copy.102), kind=kOutput, calls=%fused_computation.16 | convolution fusion | flops 537919488 | bytes 4195328 | tf_op jit(solution)/shard_map/rf,rjd->jfd/dot_general | solution.py:40
  19.0 26.8 %all-to-all-done = bf16[128,8,512]{2,1,0:T(8,128)(2,1)} async-done(((bf16[128,8,512]{2,1,0:T(8,128)(2,1)}), bf16[128,8,512]{2,1,0:T(8,128)(2,1)}, u32[]{:S(2)}, u32[]{:S(2)}) %all-to-all-start) | async-done | bytes 1048608 | tf_op jit(solution)/shard_map/all_to_all | solution.py:36
  45.8 2.3 %copy.169 = bf16[2,64,8,512]{3,2,1,0:T(8,128)(2,1)} copy(bf16[2,64,8,512]{3,2,0,1:T(8,128)(2,1)} %bitcast.3) | data formatting | bytes 2097152 | tf_op jit(solution)/shard_map/all_to_all | solution.py:36
  48.1 2.3 %copy.107 = bf16[2,512,512]{1,2,0:T(8,128)(2,1)} copy(bf16[2,512,512]{2,1,0:T(8,128)(2,1)} %bitcast.76) | data formatting | bytes 2097152 | tf_op jit(solution)/shard_map/all_to_all | solution.py:36
  50.4 2.4 %convolution_convert_fusion = bf16[2,512,512]{2,1,0:T(8,128)(2,1)S(1)} fusion(f32[2,512,512]{2,1,0:T(8,128)S(1)} %get-tuple-element.17, bf16[2,512,512]{1,2,0:T(8,128)(2,1)} %copy.107), kind=kOutput, calls=%fused_computation.21 | convolution fusion | flops 539492352 | bytes 4194304 | tf_op jit(solution)/shard_map/jfd,jgd->jfg/dot_general | solution.py:45
  52.8 17.9 %all_to_all.46 = bf16[2,4,128,512]{3,2,0,1:T(8,128)(2,1)S(1)} all-to-all(bf16[2,4,128,512]{3,2,0,1:T(8,128)(2,1)S(1)} %copy.110), channel_id=1, replica_groups=mesh['owner_0'=8,'owner_1'=4,'owner_2'=2,'col'=4] {'col'}, dimensions={1} | all-to-all | bytes 2097152 | tf_op jit(solution)/shard_map/all_to_all | solution.py:46
  70.7 0.3 reduce_sum.34
  71.0 0.2 copy.112
  71.1 1.1 broadcast_in_dim.69
  72.3 4.9 %all-to-all-start.3 = ((bf16[2,4,128,512]{2,3,0,1:T(8,128)(2,1)}), bf16[2,4,128,512]{2,3,0,1:T(8,128)(2,1)S(1)}, u32[]{:S(2)}, u32[]{:S(2)}) async-start(bf16[2,4,128,512]{2,3,0,1:T(8,128)(2,1)} %broadcast_in_dim.69), calls=%async_computation.3 | async-start | bytes 2097152 | tf_op jit(solution)/shard_map/all_to_all | solution.py:54
  77.2 0.1 select_reduce_fusion
  77.3 0.1 iota_compare_fusion
  77.5 2.1 %copy.104 = bf16[2,512,512]{2,0,1:T(2,128)(2,1)} copy(bf16[2,512,512]{1,2,0:T(8,128)(2,1)S(1)} %copy-done.4) | data formatting | bytes 2097152 | tf_op jit(solution)/shard_map/optimization_barrier | solution.py:41
  79.6 9.6 %all-to-all-done.3 = bf16[2,4,128,512]{2,3,0,1:T(8,128)(2,1)S(1)} async-done(((bf16[2,4,128,512]{2,3,0,1:T(8,128)(2,1)}), bf16[2,4,128,512]{2,3,0,1:T(8,128)(2,1)S(1)}, u32[]{:S(2)}, u32[]{:S(2)}) %all-to-all-start.3) | async-done | bytes 1048608 | tf_op jit(solution)/shard_map/all_to_all | solution.py:54
  89.2 7.3 %all-to-all-start.1 = ((bf16[2,512,512]{2,0,1:T(2,128)(2,1)}), bf16[2,512,512]{2,0,1:T(2,128)(2,1)}, u32[]{:S(2)}, u32[]{:S(2)}) async-start(bf16[2,512,512]{2,0,1:T(2,128)(2,1)} %copy.104), calls=%async_computation.1 | async-start | bytes 2097152 | tf_op jit(solution)/shard_map/all_to_all | solution.py:42
  96.5 0.5 fusion
  97.1 1.1 fusion.2
  98.2 2.3 %fusion.25 = f32[2,512,512]{2,1,0:T(8,128)} fusion(bf16[2,512,512]{1,2,0:T(8,128)(2,1)S(1)} %fusion.2, f32[2]{0:T(128)S(1)} %get-tuple-element.15, bf16[2,4,128,512]{2,3,0,1:T(8,128)(2,1)S(1)} %all-to-all-done.3), kind=kOutput, calls=%fused_computation.50 | convolution fusion | flops 538968064 | bytes 4194312 | tf_op jit(solution)/shard_map/jab,jbc->jac/dot_general | solution.py:20
  100.5 2.9 %copy.119 = f32[2,512,512]{1,2,0:T(8,128)} copy(f32[2,512,512]{2,1,0:T(8,128)} %fusion.25) | data formatting | bytes 4194304 | tf_op jit(solution)/shard_map/jab,jbc->jac/dot_general | solution.py:20
  103.4 3.3 %fusion.5 = bf16[2,512,512]{1,2,0:T(8,128)(2,1)S(1)} fusion(f32[2,512,512]{1,2,0:T(8,128)} %copy.119, bf16[2,512,512]{1,2,0:T(8,128)(2,1)S(1)} %fusion.2, f32[2,512,512]{2,1,0:T(8,128)} %fusion.25, f32[2]{0:T(128)S(1)} %get-tuple-element.15, bf16[2,4,128,512]{2,3,0,1:T(8,128)(2,1)S(1)} %all-to-all-done.3), kind=kOutput, calls=%fused_computation.11 | convolution fusion | flops 542638080 | bytes 7340040 | tf_op jit(solution)/shard_map/jab,jbc->jac/dot_general | solution.py:20
  106.7 1.7 %add_convert_fusion.1 = bf16[2,512,512]{1,2,0:T(8,128)(2,1)} fusion(bf16[2,512,512]{1,2,0:T(8,128)(2,1)S(1)} %fusion.5), kind=kOutput, calls=%fused_computation.19 | convolution fusion | flops 539492352 | bytes 2097152 | tf_op jit(solution)/shard_map/jab,jbc->jac/dot_general | solution.py:20
  108.4 5.9 %add_multiply_fusion = f32[2,512,512]{1,2,0:T(8,128)} fusion(f32[2,512,512]{2,1,0:T(8,128)S(1)} %copy-done.2, bf16[2,512,512]{1,2,0:T(8,128)(2,1)} %copy.107, f32[2]{0:T(128)S(1)} %get-tuple-element.14, bf16[2,512,512]{1,2,0:T(8,128)(2,1)} %add_convert_fusion.1, bf16[2,512,512]{1,2,0:T(8,128)(2,1)} %copy-done.5), kind=kOutput, calls=%fused_computation.17 | convolution fusion | flops 1082130432 | bytes 7340040 | tf_op jit(solution)/shard_map/jab,jbc->jac/dot_general | solution.py:20
  114.3 2.9 %copy.131 = f32[2,512,512]{2,1,0:T(8,128)} copy(f32[2,512,512]{1,2,0:T(8,128)} %add_multiply_fusion) | data formatting | bytes 4194304
  117.2 7.9 %all-to-all-done.1 = bf16[2,512,512]{2,0,1:T(2,128)(2,1)} async-done(((bf16[2,512,512]{2,0,1:T(2,128)(2,1)}), bf16[2,512,512]{2,0,1:T(2,128)(2,1)}, u32[]{:S(2)}, u32[]{:S(2)}) %all-to-all-start.1) | async-done | bytes 1048608 | tf_op jit(solution)/shard_map/all_to_all | solution.py:42
  125.1 1.4 %copy.168 = bf16[2,512,512]{2,1,0:T(8,128)(2,1)S(1)} copy(bf16[2,512,512]{2,0,1:T(2,128)(2,1)} %all-to-all-done.1) | data formatting | bytes 2097152 | tf_op jit(solution)/shard_map/all_to_all | solution.py:42
  126.5 1.1 copy.106
  127.6 2.8 %gather_fusion.1 = bf16[128,8,512]{2,1,0:T(8,128)(2,1)} fusion(bf16[128,8,512]{2,1,0:T(8,128)(2,1)} %bitcast.75, s32[1024]{0:T(1024)S(1)} %pad_clamp_fusion), kind=kCustom, calls=%fused_computation.1 | custom fusion | bytes 2097664 | tf_op jit(solution)/shard_map/gather | solution.py:74
  130.4 2.9 %convert_add_fusion = f32[128,8,512]{2,1,0:T(8,128)} fusion(bf16[128,8,512]{2,1,0:T(8,128)(2,1)} %gather_fusion.1, f32[128,8,512]{2,1,0:T(8,128)S(1)} %copy-done.3), kind=kLoop, calls=%fused_computation.20 | loop fusion | flops 1572864 | bytes 5242880 | tf_op jit(solution)/shard_map/add | solution.py:75
  (25 shorter events, 0.2 us)
Async XLA Ops:
  0.6 16.7 %copy-start = (bf16[512,512]{1,0:T(8,128)(2,1)S(1)}, bf16[512,512]{1,0:T(8,128)(2,1)}, u32[]{:S(2)}) copy-start(bf16[512,512]{1,0:T(8,128)(2,1)} %param.6) | copy-start | bytes 1572868
  1.4 15.7 %copy-start.6 = (bf16[512,512]{1,0:T(8,128)(2,1)S(1)}, bf16[512,512]{1,0:T(8,128)(2,1)}, u32[]{:S(2)}) copy-start(bf16[512,512]{1,0:T(8,128)(2,1)} %param.7) | copy-start | bytes 1572868
  4.7 12.6 %copy-start.7 = (s32[512]{0:T(512)S(1)}, s32[512]{0:T(512)}, u32[]{:S(2)}) copy-start(s32[512]{0:T(512)} %param.8) | copy-start | bytes 6148
  4.7 41.0 %all-to-all-start = ((bf16[128,8,512]{2,1,0:T(8,128)(2,1)}), bf16[128,8,512]{2,1,0:T(8,128)(2,1)}, u32[]{:S(2)}, u32[]{:S(2)}) async-start(bf16[128,8,512]{2,1,0:T(8,128)(2,1)} %gather_fusion), calls=%async_computation | async-start | bytes 2097152 | tf_op jit(solution)/shard_map/all_to_all | solution.py:36
  19.0 31.4 %copy-start.1 = (f32[2,512,512]{2,1,0:T(8,128)}, f32[2,512,512]{2,1,0:T(8,128)S(1)}, u32[]{:S(2)}) copy-start(f32[2,512,512]{2,1,0:T(8,128)S(1)} %get-tuple-element.17) | copy-start | bytes 6291460
  70.9 6.3 %copy-start.8 = (s32[128]{0:T(128)S(1)}, s32[128]{0:T(128)}, u32[]{:S(2)}) copy-start(s32[128]{0:T(128)} %param.9) | copy-start | bytes 1540
  71.0 6.5 %copy-start.4 = (bf16[2,512,512]{1,2,0:T(8,128)(2,1)S(1)}, bf16[2,512,512]{1,2,0:T(8,128)(2,1)}, u32[]{:S(2)}) copy-start(bf16[2,512,512]{1,2,0:T(8,128)(2,1)} %get-tuple-element.3) | copy-start | bytes 3145732
  72.3 17.0 %all-to-all-start.3 = ((bf16[2,4,128,512]{2,3,0,1:T(8,128)(2,1)}), bf16[2,4,128,512]{2,3,0,1:T(8,128)(2,1)S(1)}, u32[]{:S(2)}, u32[]{:S(2)}) async-start(bf16[2,4,128,512]{2,3,0,1:T(8,128)(2,1)} %broadcast_in_dim.69), calls=%async_computation.3 | async-start | bytes 2097152 | tf_op jit(solution)/shard_map/all_to_all | solution.py:54
  89.2 35.9 %all-to-all-start.1 = ((bf16[2,512,512]{2,0,1:T(2,128)(2,1)}), bf16[2,512,512]{2,0,1:T(2,128)(2,1)}, u32[]{:S(2)}, u32[]{:S(2)}) async-start(bf16[2,512,512]{2,0,1:T(2,128)(2,1)} %copy.104), calls=%async_computation.1 | async-start | bytes 2097152 | tf_op jit(solution)/shard_map/all_to_all | solution.py:42
  98.2 5.2 %copy-start.5 = (bf16[2,512,512]{1,2,0:T(8,128)(2,1)}, bf16[2,512,512]{1,2,0:T(8,128)(2,1)S(1)}, u32[]{:S(2)}) copy-start(bf16[2,512,512]{1,2,0:T(8,128)(2,1)S(1)} %fusion.2) | copy-start | bytes 3145732
  106.7 1.7 %copy-start.2 = (f32[2,512,512]{2,1,0:T(8,128)S(1)}, f32[2,512,512]{2,1,0:T(8,128)}, u32[]{:S(2)}) copy-start(f32[2,512,512]{2,1,0:T(8,128)} %copy-done.1) | copy-start | bytes 6291460
  126.5 4.0 %copy-start.3 = (f32[128,8,512]{2,1,0:T(8,128)S(1)}, f32[128,8,512]{2,1,0:T(8,128)}, u32[]{:S(2)}) copy-start(f32[128,8,512]{2,1,0:T(8,128)} %param.5) | copy-start | bytes 6291460

commit v2 on v1

v2 whole, which is shorter than its diff:
```python
import functools

import jax
import jax.numpy as jnp
from jax import lax
from jax.experimental import pallas as pl
from jax.experimental.pallas import tpu as pltpu
from jax.sharding import Mesh
from jax.sharding import PartitionSpec as P

OWNER = ("owner_0", "owner_1", "owner_2")
AXES = OWNER + ("col",)
MESH = pl.DeviceIdType.MESH

decay_rate = 0.95
epsilon = 1e-07
linear_weight = 3.4445
cubic_weight = -4.775
quintic_weight = 2.0315


def dot(a, b):
    return jnp.dot(a, b, preferred_element_type=jnp.float32)


def dot_rows(a, b):
    return lax.dot_general(a, b, (((1,), (1,)), ((), ())), preferred_element_type=jnp.float32)


def exchange_kernel(
    assign_ref,
    momentum_hbm,
    hidden_hbm,
    grads_hbm,
    routing_ref,
    back_hbm,
    update_hbm,
    mom,
    hid,
    out_grads,
    m_send,
    m_recv,
    g_send,
    upd32,
    ub,
    part,
    part_recv,
    whole_send,
    whole_recv,
    gram,
    poly,
    upd16,
    load_sem,
    own_sem,
    out_sem,
    m_ssem,
    m_rsem,
    g_ssem,
    g_rsem,
    p_ssem,
    p_rsem,
    w_ssem,
    w_rsem,
    *,
    sizes,
):
    nz, nx, nk, nc = sizes
    owners = nz * nx * nk
    rows = mom.shape[1]
    ffe = ub.shape[1]
    blk = ffe // nc
    z, x, k, c = (lax.axis_index(name) for name in AXES)
    me = (z * nx + x) * nk + k

    def peer(n):
        i = n % nz
        w = nx * nk - 1 - n // nz
        dz = nz // 2 + (i % 2) * ((i + 1) // 2) - (1 - i % 2) * (i // 2)
        pz = (z + dz) % nz
        px = (x + w // nk) % nx
        pk = (k + w % nk) % nk
        return (pz * nx + px) * nk + pk, (pz, px, pk, c)

    barrier = pltpu.get_barrier_semaphore()

    @pl.loop(0, owners - 1)
    def _(n):
        _, where = peer(n)
        pl.semaphore_signal(barrier, inc=1, device_id=where, device_id_type=MESH)

    for d in range(1, nc):
        pl.semaphore_signal(
            barrier, inc=1, device_id=(z, x, k, (c + d) % nc), device_id_type=MESH
        )

    loads = [
        pltpu.make_async_copy(momentum_hbm, mom, load_sem.at[0]),
        pltpu.make_async_copy(hidden_hbm, hid, load_sem.at[1]),
        pltpu.make_async_copy(grads_hbm, out_grads, load_sem.at[2]),
    ]
    for copy in loads:
        copy.start()
    loads[0].wait()
    for j in range(2):

        @pl.loop(0, owners, unroll=4)
        def _(o):
            m_send[j, o] = mom[assign_ref[2 * o + j]].astype(jnp.bfloat16)

    pl.semaphore_wait(barrier, owners - 1 + nc - 1)

    for j in range(2):

        @pl.loop(0, owners - 1)
        def _(n):
            to, where = peer(n)
            pltpu.make_async_remote_copy(
                src_ref=m_send.at[j, to],
                dst_ref=m_recv.at[j, me],
                send_sem=m_ssem.at[j],
                recv_sem=m_rsem.at[j],
                device_id=where,
                device_id_type=MESH,
            ).start()

    loads[1].wait()
    loads[2].wait()
    hid_t = hid[...].T
    for j in range(2):
        m_recv[j, me] = m_send[j, me]
        chosen = jnp.where(routing_ref[...] == j, hid_t, jnp.zeros((), jnp.bfloat16))
        upd32[j] = dot(chosen, out_grads[...])

        @pl.loop(0, owners, unroll=4)
        def _(o):
            at = pl.multiple_of(o * rows, rows)
            g_send[j, o] = upd32[j, pl.ds(at, rows), :].astype(jnp.bfloat16)

    own = []
    for j in range(2):
        copy = pltpu.make_async_copy(g_send.at[j, me], back_hbm.at[j, me], own_sem.at[j])
        copy.start()
        own.append(copy)

        @pl.loop(0, owners - 1)
        def _(n):
            to, where = peer(n)
            pltpu.make_async_remote_copy(
                src_ref=g_send.at[j, to],
                dst_ref=back_hbm.at[j, me],
                send_sem=g_ssem.at[j],
                recv_sem=g_rsem.at[j],
                device_id=where,
                device_id_type=MESH,
            ).start()

    def spread(source, target, send, recv, j):
        for d in range(1, nc):
            to = (c + d) % nc
            pltpu.make_async_remote_copy(
                src_ref=source(to),
                dst_ref=target,
                send_sem=send.at[j],
                recv_sem=recv.at[j],
                device_id=(z, x, k, to),
                device_id_type=MESH,
            ).start()

    def arrived(ref, sem):
        pltpu.make_async_copy(ref, ref, sem).wait()

    def partial_gram(j):
        arrived(m_recv.at[j, pl.ds(0, owners - 1)], m_rsem.at[j])

        @pl.loop(0, owners, unroll=4)
        def _(o):
            at = pl.multiple_of(o * rows, rows)
            upd32[j, pl.ds(at, rows), :] = decay_rate * m_recv[j, o].astype(
                jnp.float32
            ) + upd32[j, pl.ds(at, rows), :]

        ub[j] = upd32[j].astype(jnp.bfloat16)
        product = dot_rows(ub[j], ub[j])
        for b in range(nc):
            for t in range(3):
                at = (b + t) % nc * blk
                part[j, b, t] = product[b * blk : (b + 1) * blk, at : at + blk].astype(jnp.bfloat16)
        spread(lambda to: part.at[j, to], part_recv.at[j, c], p_ssem, p_rsem, j)
        part_recv[j, c] = part[j, c]

    def sum_parts(j):
        arrived(part_recv.at[j, pl.ds(0, nc - 1)], p_rsem.at[j])
        total = part_recv[j, 0].astype(jnp.float32)
        for b in range(1, nc):
            total = total + part_recv[j, b].astype(jnp.float32)
        whole_send[j] = total.astype(jnp.bfloat16)
        spread(lambda to: whole_send.at[j], whole_recv.at[j, c], w_ssem, w_rsem, j)
        whole_recv[j, c] = whole_send[j]

    partial_gram(0)
    sum_parts(0)
    partial_gram(1)

    @pl.loop(0, 2)
    def _(j):
        arrived(whole_recv.at[j, pl.ds(0, nc - 1)], w_rsem.at[j])
        eye = lax.broadcasted_iota(jnp.int32, (blk, blk), 0) == lax.broadcasted_iota(
            jnp.int32, (blk, blk), 1
        )
        diagonal = jnp.zeros((blk, blk), jnp.float32)
        for b in range(nc):
            diagonal = diagonal + jnp.where(eye, whole_recv[j, b, 0].astype(jnp.float32), 0.0)
        squares = jnp.sum(
            jnp.sum(diagonal, axis=0, keepdims=True), axis=1, keepdims=True
        )
        inverse = 1.0 / (jnp.sqrt(squares) + epsilon)
        for b in range(nc):
            for t in range(3):
                at = (b + t) % nc * blk
                block = (whole_recv[j, b, t].astype(jnp.float32) * inverse) * inverse
                gram[b * blk : (b + 1) * blk, at : at + blk] = block.astype(jnp.bfloat16)
                if t == 1:
                    gram[at : at + blk, b * blk : (b + 1) * blk] = block.T.astype(jnp.bfloat16)
        g1 = gram[...]
        p1 = (cubic_weight * g1.astype(jnp.float32) + quintic_weight * dot(g1, g1)).astype(
            jnp.bfloat16
        )
        poly[...] = p1
        t1 = dot(g1, p1)
        g2 = (
            linear_weight**2 * g1.astype(jnp.float32)
            + 2.0 * linear_weight * t1
            + dot(p1, t1.astype(jnp.bfloat16))
        ).astype(jnp.bfloat16)
        gram[...] = g2
        p2 = (cubic_weight * g2.astype(jnp.float32) + quintic_weight * dot(g2, g2)).astype(
            jnp.bfloat16
        )
        p1 = poly[...]
        rest = (
            linear_weight * (p1.astype(jnp.float32) + p2.astype(jnp.float32)) + dot(p2, p1)
        ).astype(jnp.bfloat16)
        upd16[j] = (
            inverse * (linear_weight**2 * upd32[j] + dot(rest, ub[j]))
        ).astype(jnp.bfloat16)
        pltpu.make_async_copy(upd16.at[j], update_hbm.at[j], out_sem.at[j]).start()

        @pl.when(j == 0)
        def _():
            sum_parts(1)

    for j in range(2):
        pltpu.make_async_copy(upd16.at[j], update_hbm.at[j], out_sem.at[j]).wait()
        arrived(m_send.at[j, pl.ds(0, owners - 1)], m_ssem.at[j])
        arrived(part.at[j, pl.ds(0, nc - 1)], p_ssem.at[j])
        arrived(whole_recv.at[j, pl.ds(0, nc - 1)], w_ssem.at[j])
        own[j].wait()
    for j in range(2):
        arrived(g_send.at[j, pl.ds(0, owners - 1)], g_ssem.at[j])
        arrived(back_hbm.at[j, pl.ds(0, owners - 1)], g_rsem.at[j])


def finish_kernel(
    assign_ref,
    momentum_hbm,
    back_hbm,
    update_hbm,
    new_hbm,
    out_hbm,
    mom,
    back,
    upd16,
    new,
    upd32,
    place,
    mom_sem,
    back_sem,
    upd_sem,
    new_sem,
    out_sem,
    *,
    scaling,
):
    experts = mom.shape[0]
    chunks = mom_sem.shape[0]
    step = experts // chunks
    owners = back.shape[1]
    back_copy = pltpu.make_async_copy(back_hbm, back, back_sem.at[0])
    back_copy.start()
    mom_copies, upd_copies, outs = [], [], []
    for q in range(chunks):
        part = pl.ds(q * step, step)
        copy = pltpu.make_async_copy(momentum_hbm.at[part], mom.at[part], mom_sem.at[q])
        copy.start()
        mom_copies.append(copy)
    for j in range(2):
        copy = pltpu.make_async_copy(update_hbm.at[j], upd16.at[j], upd_sem.at[j])
        copy.start()
        upd_copies.append(copy)

    @pl.loop(0, owners, unroll=4)
    def _(o):
        for j in range(2):
            place[assign_ref[2 * o + j]] = j * owners + o

    back_copy.wait()
    for q in range(chunks):
        mom_copies[q].wait()

        @pl.loop(q * step, (q + 1) * step, unroll=4)
        def _(e):
            at = place[e]
            new[e] = decay_rate * mom[e] + back[at // owners, at % owners].astype(jnp.float32)

        part = pl.ds(q * step, step)
        copy = pltpu.make_async_copy(new.at[part], new_hbm.at[part], new_sem.at[q])
        copy.start()
        outs.append(copy)
    for j in range(2):
        upd_copies[j].wait()
        upd32[j] = scaling * upd16[j].astype(jnp.float32)
        copy = pltpu.make_async_copy(upd32.at[j], out_hbm.at[j], out_sem.at[j])
        copy.start()
        outs.append(copy)
    for copy in outs:
        copy.wait()


def body(momentum, hidden_acts, output_grads, routing, assignment):
    sizes = tuple(lax.axis_size(name) for name in AXES)
    owners = sizes[0] * sizes[1] * sizes[2]
    nc = sizes[3]
    experts, rows, cols = momentum.shape
    tokens, ffe = hidden_acts.shape
    width = cols * nc
    blk = ffe // nc
    scaling = 0.2 * float(max(ffe, width)) ** 0.5
    bf16, f32 = jnp.bfloat16, jnp.float32
    anywhere = pl.BlockSpec(memory_space=pl.ANY)
    smem = pl.BlockSpec(memory_space=pltpu.SMEM)
    vmem = pl.BlockSpec(memory_space=pltpu.VMEM)
    sem = pltpu.SemaphoreType.DMA
    back, update = pl.pallas_call(
        functools.partial(exchange_kernel, sizes=sizes),
        out_shape=(
            jax.ShapeDtypeStruct((2, owners, rows, cols), bf16),
            jax.ShapeDtypeStruct((2, ffe, cols), bf16),
        ),
        in_specs=[smem, anywhere, anywhere, anywhere, vmem],
        out_specs=(anywhere, anywhere),
        scratch_shapes=[
            pltpu.VMEM((experts, rows, cols), f32),
            pltpu.VMEM((tokens, ffe), bf16),
            pltpu.VMEM((tokens, cols), bf16),
            pltpu.VMEM((2, owners, rows, cols), bf16),
            pltpu.VMEM((2, owners, rows, cols), bf16),
            pltpu.VMEM((2, owners, rows, cols), bf16),
            pltpu.VMEM((2, ffe, cols), f32),
            pltpu.VMEM((2, ffe, cols), bf16),
            pltpu.VMEM((2, nc, 3, blk, blk), bf16),
            pltpu.VMEM((2, nc, 3, blk, blk), bf16),
            pltpu.VMEM((2, 3, blk, blk), bf16),
            pltpu.VMEM((2, nc, 3, blk, blk), bf16),
            pltpu.VMEM((ffe, ffe), bf16),
            pltpu.VMEM((ffe, ffe), bf16),
            pltpu.VMEM((2, ffe, cols), bf16),
            sem((3,)),
            sem((2,)),
            sem((2,)),
            sem((2,)),
            sem((2,)),
            sem((2,)),
            sem((2,)),
            sem((2,)),
            sem((2,)),
            sem((2,)),
            sem((2,)),
        ],
        compiler_params=pltpu.CompilerParams(collective_id=0, has_side_effects=True),
        name="exchange",
    )(assignment, momentum, hidden_acts, output_grads, routing.reshape(1, tokens))
    chunks = 4
    return pl.pallas_call(
        functools.partial(finish_kernel, scaling=scaling),
        out_shape=(
            jax.ShapeDtypeStruct((experts, rows, cols), f32),
            jax.ShapeDtypeStruct((2, ffe, cols), f32),
        ),
        in_specs=[smem, anywhere, anywhere, anywhere],
        out_specs=(anywhere, anywhere),
        scratch_shapes=[
            pltpu.VMEM((experts, rows, cols), f32),
            pltpu.VMEM((2, owners, rows, cols), bf16),
            pltpu.VMEM((2, ffe, cols), bf16),
            pltpu.VMEM((experts, rows, cols), f32),
            pltpu.VMEM((2, ffe, cols), f32),
            pltpu.SMEM((experts,), jnp.int32),
            sem((chunks,)),
            sem((1,)),
            sem((2,)),
            sem((chunks,)),
            sem((2,)),
        ],
        name="finish",
    )(assignment, momentum, back, update)


def solution(mesh):
    owners = mesh.shape["owner"]
    cores = 2 if owners % 2 == 0 else 1
    across = 4 if owners % 8 == 0 else 1
    torus = Mesh(
        mesh.devices.reshape(owners // (across * cores), across, cores, mesh.shape["col"]), AXES
    )
    return jax.shard_map(
        body,
        mesh=torus,
        in_specs=(P(None, OWNER, "col"), P(OWNER, None), P(OWNER, "col"), P(OWNER), P()),
        out_specs=(P(None, OWNER, "col"), P(OWNER, None, "col")),
        check_vma=False,
    )
```

time: 135 us -> 65.8 us (0.49)
  Pallas kernels: 0 us -> 64.6 us
  waiting for transfers between devices: 44.3 us -> 0 us
  starting transfers between devices: 24.6 us -> 0 us
  local copies, waits for them, and re-layouts: 22.8 us -> 0 us
  matrix products: 18.3 us -> 0 us
  blocking collectives: 17.9 us -> 0 us
  other arithmetic: 4.65 us -> 0 us
    pallas_call x0 -> x2, Pallas kernels: none -> 64.6 us  [the longest x1 59.4 us: body(): pl.pallas_call(functools.partial(exchange_kernel, sizes=sizes), out_shape...]
    all_to_all x3 -> x0, waiting for transfers between devices: 44.3 us -> none  [the longest x1 26.8 us: body(): lax.all_to_all(ordered, OWNER, split_axis=0, concat_axis=1, tiled=True)]
    all_to_all x3 -> x0, starting transfers between devices: 24.6 us -> none  [the longest x1 12.3 us: body(): lax.all_to_all(ordered, OWNER, split_axis=0, concat_axis=1, tiled=True)]
    dot_general x7 -> x0, matrix products: 18.3 us -> none  [the longest x5 14.2 us: mm(): jnp.einsum('jab,jbc->jac', a.astype(jnp.bfloat16), b.astype(jnp.bfloat16)...]
    all_to_all x1 -> x0, blocking collectives: 17.9 us -> none  [body(): lax.all_to_all(partial.astype(jnp.bfloat16).reshape(EXP_DEV, n_col, FFE /...]
    all_to_all x4 -> x0, local copies, waits for them, and re-layouts: 7.12 us -> none  [the longest x2 4.6 us: body(): lax.all_to_all(ordered, OWNER, split_axis=0, concat_axis=1, tiled=True)]
    gather x2 -> x0, local copies, waits for them, and re-layouts: 6.18 us -> none  [the longest x1 3.35 us: body(): momentum.at[assignment].get(mode='promise_in_bounds').astype(jnp.bfloat16)]
    unnamed x20 -> x0, local copies, waits for them, and re-layouts: 3.14 us -> none
  transfers between devices with their start and end apart: 3 -> 0, of which waited for: 3 -> 0; matrix products, arithmetic and copies ran while one was open for 19% -> 0% of each run, Pallas kernels for 0% -> 0%
where the time goes in v2:
time: 65.8 us; the launch traced here: 65.3 us
  Pallas kernels  64.6 us (98%)
    pallas_call x1, Pallas kernels, body(): pl.pallas_call(functools.partial(exchange_kernel, sizes=sizes), out_shape...  59.4 us
    pallas_call x1, Pallas kernels, body(): pl.pallas_call(functools.partial(finish_kernel, scaling=scaling), out_sha...  5.27 us

profile of v2, /device:TPU:8, one launch (start us, length us, event | category | flops | bytes accessed | tf_op | source)
XLA Modules:
  0.0 65.3 jit_solution(7402037368790467077)
XLA Ops:
  0.6 59.4 %exchange.1 = (bf16[2,64,8,512]{3,2,1,0:T(8,128)(2,1)}, bf16[2,512,512]{2,1,0:T(8,128)(2,1)}) custom-call(s32[128]{0:T(128)} %assign_ref.3, f32[128,8,512]{2,1,0:T(8,128)} %momentum_hbm.3, bf16[512,512]{1,0:T(8,128)(2,1)} %hidden_hbm.1, bf16[512,512]{1,0:T(8,128)(2,1)} %grads_hbm.1, s32[1,512]{1,0:T(1,128)} %bitcast.1), custom_call_target="tpu_custom_call" | custom-call | tf_op jit(solution)/shard_map/exchange/pallas_call | solution.py:343
  60.0 5.3 %finish.1 = (f32[128,8,512]{2,1,0:T(8,128)}, f32[2,512,512]{2,1,0:T(8,128)}) custom-call(s32[128]{0:T(128)} %assign_ref.3, f32[128,8,512]{2,1,0:T(8,128)} %momentum_hbm.3, bf16[2,64,8,512]{3,2,1,0:T(8,128)(2,1)} %get-tuple-element.4.back_hbm, bf16[2,512,512]{2,1,0:T(8,128)(2,1)} %get-tuple-element.5.update_hbm), custom_call_target="tpu_custom_call" | custom-call | tf_op jit(solution)/shard_map/finish/pallas_call | solution.py:383

commit v3 on v2

--- a/solution.py
+++ b/solution.py
@@ -33,14 +33,15 @@
     hidden_hbm,
     grads_hbm,
     routing_ref,
-    back_hbm,
-    update_hbm,
+    new_ref,
+    update_ref,
     mom,
     hid,
     out_grads,
     m_send,
     m_recv,
     g_send,
+    g_recv,
     upd32,
     ub,
     part,
@@ -49,10 +50,7 @@
     whole_recv,
     gram,
     poly,
-    upd16,
     load_sem,
-    own_sem,
-    out_sem,
     m_ssem,
     m_rsem,
     g_ssem,
@@ -63,6 +61,7 @@
     w_rsem,
     *,
     sizes,
+    scaling,
 ):
     nz, nx, nk, nc = sizes
     owners = nz * nx * nk
@@ -72,14 +71,20 @@
     z, x, k, c = (lax.axis_index(name) for name in AXES)
     me = (z * nx + x) * nk + k
 
-    def peer(n):
+    def offsets(n):
         i = n % nz
         w = nx * nk - 1 - n // nz
         dz = nz // 2 + (i % 2) * ((i + 1) // 2) - (1 - i % 2) * (i // 2)
-        pz = (z + dz) % nz
-        px = (x + w // nk) % nx
-        pk = (k + w % nk) % nk
+        return dz, w // nk, w % nk
+
+    def peer(n):
+        dz, dx, dk = offsets(n)
+        pz, px, pk = (z + dz) % nz, (x + dx) % nx, (k + dk) % nk
         return (pz * nx + px) * nk + pk, (pz, px, pk, c)
+
+    def sender(n):
+        dz, dx, dk = offsets(n)
+        return (((z + nz - dz) % nz) * nx + (x + nx - dx) % nx) * nk + (k + nk - dk) % nk
 
     barrier = pltpu.get_barrier_semaphore()
 
@@ -134,25 +139,21 @@
         @pl.loop(0, owners, unroll=4)
         def _(o):
             at = pl.multiple_of(o * rows, rows)
-            g_send[j, o] = upd32[j, pl.ds(at, rows), :].astype(jnp.bfloat16)
-
-    own = []
-    for j in range(2):
-        copy = pltpu.make_async_copy(g_send.at[j, me], back_hbm.at[j, me], own_sem.at[j])
-        copy.start()
-        own.append(copy)
-
-        @pl.loop(0, owners - 1)
-        def _(n):
-            to, where = peer(n)
-            pltpu.make_async_remote_copy(
-                src_ref=g_send.at[j, to],
-                dst_ref=back_hbm.at[j, me],
-                send_sem=g_ssem.at[j],
-                recv_sem=g_rsem.at[j],
-                device_id=where,
-                device_id_type=MESH,
-            ).start()
+            g_send[o, j] = upd32[j, pl.ds(at, rows), :].astype(jnp.bfloat16)
+
+    @pl.loop(0, owners - 1)
+    def _(n):
+        to, where = peer(n)
+        pltpu.make_async_remote_copy(
+            src_ref=g_send.at[to],
+            dst_ref=g_recv.at[me],
+            send_sem=g_ssem,
+            recv_sem=g_rsem.at[n // nz],
+            device_id=where,
+            device_id_type=MESH,
+        ).start()
+
+    g_recv[me] = g_send[me]
 
     def spread(source, target, send, recv, j):
         for d in range(1, nc):
@@ -240,90 +241,48 @@
         rest = (
             linear_weight * (p1.astype(jnp.float32) + p2.astype(jnp.float32)) + dot(p2, p1)
         ).astype(jnp.bfloat16)
-        upd16[j] = (
-            inverse * (linear_weight**2 * upd32[j] + dot(rest, ub[j]))
-        ).astype(jnp.bfloat16)
-        pltpu.make_async_copy(upd16.at[j], update_hbm.at[j], out_sem.at[j]).start()
+        turned = (inverse * (linear_weight**2 * upd32[j] + dot(rest, ub[j]))).astype(jnp.bfloat16)
+        update_ref[j] = scaling * turned.astype(jnp.float32)
 
         @pl.when(j == 0)
         def _():
             sum_parts(1)
 
+    def combine(q):
+        for i in range(nz):
+            o = sender(q * nz + i)
+            for j in range(2):
+                new_ref[2 * o + j] = decay_rate * mom[assign_ref[2 * o + j]] + g_recv[o, j].astype(
+                    jnp.float32
+                )
+
+    groups = owners // nz
+
+    @pl.loop(0, groups - 1)
+    def _(q):
+        arrived(g_recv.at[pl.ds(0, nz)], g_rsem.at[q])
+        combine(q)
+
+    arrived(g_recv.at[pl.ds(0, nz - 1)], g_rsem.at[groups - 1])
+    combine(groups - 1)
+
     for j in range(2):
-        pltpu.make_async_copy(upd16.at[j], update_hbm.at[j], out_sem.at[j]).wait()
         arrived(m_send.at[j, pl.ds(0, owners - 1)], m_ssem.at[j])
         arrived(part.at[j, pl.ds(0, nc - 1)], p_ssem.at[j])
         arrived(whole_recv.at[j, pl.ds(0, nc - 1)], w_ssem.at[j])
-        own[j].wait()
-    for j in range(2):
-        arrived(g_send.at[j, pl.ds(0, owners - 1)], g_ssem.at[j])
-        arrived(back_hbm.at[j, pl.ds(0, owners - 1)], g_rsem.at[j])
-
-
-def finish_kernel(
-    assign_ref,
-    momentum_hbm,
-    back_hbm,
-    update_hbm,
-    new_hbm,
-    out_hbm,
-    mom,
-    back,
-    upd16,
-    new,
-    upd32,
-    place,
-    mom_sem,
-    back_sem,
-    upd_sem,
-    new_sem,
-    out_sem,
-    *,
-    scaling,
-):
-    experts = mom.shape[0]
-    chunks = mom_sem.shape[0]
-    step = experts // chunks
-    owners = back.shape[1]
-    back_copy = pltpu.make_async_copy(back_hbm, back, back_sem.at[0])
-    back_copy.start()
-    mom_copies, upd_copies, outs = [], [], []
-    for q in range(chunks):
-        part = pl.ds(q * step, step)
-        copy = pltpu.make_async_copy(momentum_hbm.at[part], mom.at[part], mom_sem.at[q])
-        copy.start()
-        mom_copies.append(copy)
-    for j in range(2):
-        copy = pltpu.make_async_copy(update_hbm.at[j], upd16.at[j], upd_sem.at[j])
-        copy.start()
-        upd_copies.append(copy)
-
-    @pl.loop(0, owners, unroll=4)
-    def _(o):
-        for j in range(2):
-            place[assign_ref[2 * o + j]] = j * owners + o
-
-    back_copy.wait()
-    for q in range(chunks):
-        mom_copies[q].wait()
-
-        @pl.loop(q * step, (q + 1) * step, unroll=4)
-        def _(e):
-            at = place[e]
-            new[e] = decay_rate * mom[e] + back[at // owners, at % owners].astype(jnp.float32)
-
-        part = pl.ds(q * step, step)
-        copy = pltpu.make_async_copy(new.at[part], new_hbm.at[part], new_sem.at[q])
-        copy.start()
-        outs.append(copy)
-    for j in range(2):
-        upd_copies[j].wait()
-        upd32[j] = scaling * upd16[j].astype(jnp.float32)
-        copy = pltpu.make_async_copy(upd32.at[j], out_hbm.at[j], out_sem.at[j])
-        copy.start()
-        outs.append(copy)
-    for copy in outs:
-        copy.wait()
+    arrived(g_send.at[pl.ds(0, owners - 1)], g_ssem)
+
+
+def place_kernel(assign_ref, new_ref, update_ref, new_hbm, out_hbm, new_sem, out_sem):
+    copy = pltpu.make_async_copy(update_ref, out_hbm, out_sem)
+    copy.start()
+
+    @pl.loop(0, new_ref.shape[0], unroll=8)
+    def _(s):
+        pltpu.make_async_copy(new_ref.at[s], new_hbm.at[assign_ref[s]], new_sem).start()
+
+    copy.wait()
+    pltpu.make_async_copy(new_ref, new_hbm, new_sem).wait()
 
 
 def body(momentum, hidden_acts, output_grads, routing, assignment):
@@ -336,25 +295,26 @@
     blk = ffe // nc
     scaling = 0.2 * float(max(ffe, width)) ** 0.5
     bf16, f32 = jnp.bfloat16, jnp.float32
-    anywhere = pl.BlockSpec(memory_space=pl.ANY)
+    hbm = pl.BlockSpec(memory_space=pltpu.HBM)
     smem = pl.BlockSpec(memory_space=pltpu.SMEM)
     vmem = pl.BlockSpec(memory_space=pltpu.VMEM)
     sem = pltpu.SemaphoreType.DMA
-    back, update = pl.pallas_call(
-        functools.partial(exchange_kernel, sizes=sizes),
+    placed, update = pl.pallas_call(
+        functools.partial(exchange_kernel, sizes=sizes, scaling=scaling),
         out_shape=(
-            jax.ShapeDtypeStruct((2, owners, rows, cols), bf16),
-            jax.ShapeDtypeStruct((2, ffe, cols), bf16),
+            pltpu.VMEM((experts, rows, cols), f32),
+            pltpu.VMEM((2, ffe, cols), f32),
         ),
-        in_specs=[smem, anywhere, anywhere, anywhere, vmem],
-        out_specs=(anywhere, anywhere),
+        in_specs=[smem, hbm, hbm, hbm, vmem],
+        out_specs=(vmem, vmem),
         scratch_shapes=[
             pltpu.VMEM((experts, rows, cols), f32),
             pltpu.VMEM((tokens, ffe), bf16),
             pltpu.VMEM((tokens, cols), bf16),
             pltpu.VMEM((2, owners, rows, cols), bf16),
             pltpu.VMEM((2, owners, rows, cols), bf16),
-            pltpu.VMEM((2, owners, rows, cols), bf16),
+            pltpu.VMEM((owners, 2, rows, cols), bf16),
+            pltpu.VMEM((owners, 2, rows, cols), bf16),
             pltpu.VMEM((2, ffe, cols), f32),
             pltpu.VMEM((2, ffe, cols), bf16),
             pltpu.VMEM((2, nc, 3, blk, blk), bf16),
@@ -363,46 +323,43 @@
             pltpu.VMEM((2, nc, 3, blk, blk), bf16),
             pltpu.VMEM((ffe, ffe), bf16),
             pltpu.VMEM((ffe, ffe), bf16),
-            pltpu.VMEM((2, ffe, cols), bf16),
             sem((3,)),
             sem((2,)),
             sem((2,)),
-            sem((2,)),
-            sem((2,)),
-            sem((2,)),
-            sem((2,)),
+            sem(()),
+            sem((owners // sizes[0],)),
             sem((2,)),
             sem((2,)),
             sem((2,)),
             sem((2,)),
         ],
-        compiler_params=pltpu.CompilerParams(collective_id=0, has_side_effects=True),
+        compiler_params=pltpu.CompilerParams(
+            collective_id=0, has_side_effects=True, vmem_limit_bytes=36 << 20
+        ),
         name="exchange",
-    )(assignment, momentum, hidden_acts, output_grads, routing.reshape(1, tokens))
-    chunks = 4
+    )(
+        pltpu.with_memory_space_constraint(assignment, pltpu.HBM),
+        pltpu.with_memory_space_constraint(momentum, pltpu.HBM),
+        pltpu.with_memory_space_constraint(hidden_acts, pltpu.HBM),
+        pltpu.with_memory_space_constraint(output_grads, pltpu.HBM),
+        pltpu.with_memory_space_constraint(routing.reshape(1, tokens), pltpu.HBM),
+    )
     return pl.pallas_call(
-        functools.partial(finish_kernel, scaling=scaling),
+        place_kernel,
         out_shape=(
             jax.ShapeDtypeStruct((experts, rows, cols), f32),
             jax.ShapeDtypeStruct((2, ffe, cols), f32),
         ),
-        in_specs=[smem, anywhere, anywhere, anywhere],
-        out_specs=(anywhere, anywhere),
-        scratch_shapes=[
-            pltpu.VMEM((experts, rows, cols), f32),
-            pltpu.VMEM((2, owners, rows, cols), bf16),
-            pltpu.VMEM((2, ffe, cols), bf16),
-            pltpu.VMEM((experts, rows, cols), f32),
-            pltpu.VMEM((2, ffe, cols), f32),
-            pltpu.SMEM((experts,), jnp.int32),
-            sem((chunks,)),
-            sem((1,)),
-            sem((2,)),
-            sem((chunks,)),
-            sem((2,)),
-        ],
-        name="finish",
-    )(assignment, momentum, back, update)
+        in_specs=[smem, vmem, vmem],
+        out_specs=(hbm, hbm),
+        scratch_shapes=[sem(()), sem(())],
+        compiler_params=pltpu.CompilerParams(vmem_limit_bytes=4 << 20),
+        name="place",
+    )(
+        assignment,
+        pltpu.with_memory_space_constraint(placed, pltpu.VMEM),
+        pltpu.with_memory_space_constraint(update, pltpu.VMEM),
+    )
 
 
 def solution(mesh):

time: 65.8 us -> 62.4 us (0.948)
  Pallas kernels: 64.6 us -> 61.5 us
    pallas_call x2, Pallas kernels: 64.6 us -> 61.5 us  [the longest x1 59 us: body(): pl.pallas_call(functools.partial(exchange_kernel, sizes=sizes, scaling=sc...]
where the time goes in v3:
time: 62.4 us; the launch traced here: 62.2 us
  Pallas kernels  61.5 us (99%)
  between operations  0.65 us (1%)
    pallas_call x1, Pallas kernels, body(): pl.pallas_call(functools.partial(exchange_kernel, sizes=sizes, scaling=sc...  59 us
    pallas_call x1, Pallas kernels, body(): pl.pallas_call(place_kernel, out_shape=(jax.ShapeDtypeStruct((experts, ro...  2.52 us

profile of v3, /device:TPU:8, one launch (start us, length us, event | category | flops | bytes accessed | tf_op | source)
XLA Modules:
  0.0 62.2 jit_solution(4559746875207011366)
XLA Ops:
  0.6 0.0 copy-start
  0.6 59.0 %exchange.1 = (f32[128,8,512]{2,1,0:T(8,128)S(1)}, f32[2,512,512]{2,1,0:T(8,128)S(1)}) custom-call(s32[128]{0:T(128)} %assign_ref.3, f32[128,8,512]{2,1,0:T(8,128)} %momentum_hbm.1, bf16[512,512]{1,0:T(8,128)(2,1)} %hidden_hbm.1, bf16[512,512]{1,0:T(8,128)(2,1)} %grads_hbm.1, s32[1,512]{1,0:T(1,128)} %bitcast.1), custom_call_target="tpu_custom_call" | custom-call | tf_op jit(solution)/shard_map/exchange/pallas_call | solution.py:302
  59.6 0.0 copy-done
  59.7 2.5 %place.1 = (f32[128,8,512]{2,1,0:T(8,128)}, f32[2,512,512]{2,1,0:T(8,128)}) custom-call(s32[128]{0:T(128)S(1)} %copy-done, f32[128,8,512]{2,1,0:T(8,128)S(1)} %get-tuple-element.4.new_ref, f32[2,512,512]{2,1,0:T(8,128)S(1)} %get-tuple-element.5.update_ref), custom_call_target="tpu_custom_call" | custom-call | tf_op jit(solution)/shard_map/place/pallas_call | solution.py:347
Async XLA Ops:
  0.6 59.0 %copy-start = (s32[128]{0:T(128)S(1)}, s32[128]{0:T(128)}, u32[]{:S(2)}) copy-start(s32[128]{0:T(128)} %assign_ref.3) | copy-start | bytes 1540

commit v4 on v3

--- a/solution.py
+++ b/solution.py
@@ -50,6 +50,7 @@
     whole_recv,
     gram,
     poly,
+    hop_sem,
     load_sem,
     m_ssem,
     m_rsem,
@@ -86,16 +87,24 @@
         dz, dx, dk = offsets(n)
         return (((z + nz - dz) % nz) * nx + (x + nx - dx) % nx) * nk + (k + nk - dk) % nk
 
+    zs = [lax.rem(z + d, nz) for d in range(nz)]
+    xs = [lax.rem(x + d, nx) for d in range(nx)]
+    ks = [lax.rem(k + d, nk) for d in range(nk)]
+    above, below = (zs[1], x, k, c), (zs[nz - 1], x, k, c)
     barrier = pltpu.get_barrier_semaphore()
-
-    @pl.loop(0, owners - 1)
-    def _(n):
-        _, where = peer(n)
-        pl.semaphore_signal(barrier, inc=1, device_id=where, device_id_type=MESH)
-
+    for dx in sorted(range(nx), key=lambda d: -min(d, nx - d)):
+        for dk in range(nk - 1, -1, -1):
+            for dz in (1, nz - 1, 0):
+                if (dz, dx, dk) != (0, 0, 0):
+                    pl.semaphore_signal(
+                        barrier,
+                        inc=1,
+                        device_id=(zs[dz], xs[dx], ks[dk], c),
+                        device_id_type=MESH,
+                    )
     for d in range(1, nc):
         pl.semaphore_signal(
-            barrier, inc=1, device_id=(z, x, k, (c + d) % nc), device_id_type=MESH
+            barrier, inc=1, device_id=(z, x, k, lax.rem(c + d, nc)), device_id_type=MESH
         )
 
     loads = [
@@ -106,27 +115,44 @@
     for copy in loads:
         copy.start()
     loads[0].wait()
-    for j in range(2):
-
+    def convert(j):
         @pl.loop(0, owners, unroll=4)
         def _(o):
             m_send[j, o] = mom[assign_ref[2 * o + j]].astype(jnp.bfloat16)
 
-    pl.semaphore_wait(barrier, owners - 1 + nc - 1)
-
-    for j in range(2):
-
-        @pl.loop(0, owners - 1)
-        def _(n):
-            to, where = peer(n)
-            pltpu.make_async_remote_copy(
-                src_ref=m_send.at[j, to],
-                dst_ref=m_recv.at[j, me],
-                send_sem=m_ssem.at[j],
-                recv_sem=m_rsem.at[j],
-                device_id=where,
-                device_id_type=MESH,
-            ).start()
+    def send_planes(j, planes, first=0):
+        @pl.loop(first, nx * nk)
+        def _(w):
+            px, pk = lax.rem(x + w // nk, nx), lax.rem(k + w % nk, nk)
+            for dz in planes:
+                pltpu.make_async_remote_copy(
+                    src_ref=m_send.at[j, (zs[dz] * nx + px) * nk + pk],
+                    dst_ref=m_recv.at[j, me],
+                    send_sem=m_ssem.at[j],
+                    recv_sem=m_rsem.at[j],
+                    device_id=(zs[dz], px, pk, c),
+                    device_id_type=MESH,
+                ).start()
+
+    convert(0)
+    pl.semaphore_wait(barrier, 3 * nx * nk - 1 + nc - 1)
+    half = nz // 2
+    for d in range(1, half + 1):
+        if d > 1:
+            pl.semaphore_wait(hop_sem.at[d - 2], 2)
+        if d < half:
+            for where in (above, below):
+                pl.semaphore_signal(
+                    hop_sem.at[d - 1], inc=1, device_id=where, device_id_type=MESH
+                )
+        send_planes(0, [d] if d == half else [d, nz - d])
+    send_planes(0, [0], 1)
+    convert(1)
+    order = [half]
+    for d in range(half - 1, 0, -1):
+        order += [nz - d, d]
+    send_planes(1, order)
+    send_planes(1, [0], 1)
 
     loads[1].wait()
     loads[2].wait()
@@ -323,6 +349,7 @@
             pltpu.VMEM((2, nc, 3, blk, blk), bf16),
             pltpu.VMEM((ffe, ffe), bf16),
             pltpu.VMEM((ffe, ffe), bf16),
+            pltpu.SemaphoreType.REGULAR((sizes[0] // 2 - 1,)),
             sem((3,)),
             sem((2,)),
             sem((2,)),

time: 62.4 us -> 60 us (0.962)
  Pallas kernels: 61.5 us -> 59.2 us
    pallas_call x1, Pallas kernels: 59 us -> 56.7 us  [body(): pl.pallas_call(functools.partial(exchange_kernel, sizes=sizes, scaling=sc...]
where the time goes in v4:
time: 60 us; the launch traced here: 59.8 us
  Pallas kernels  59.2 us (99%)
  between operations  0.65 us (1%)
    pallas_call x1, Pallas kernels, body(): pl.pallas_call(functools.partial(exchange_kernel, sizes=sizes, scaling=sc...  56.7 us
    pallas_call x1, Pallas kernels, body(): pl.pallas_call(place_kernel, out_shape=(jax.ShapeDtypeStruct((experts, ro...  2.52 us

profile of v4, /device:TPU:8, one launch (start us, length us, event | category | flops | bytes accessed | tf_op | source)
XLA Modules:
  0.0 59.8 jit_solution(17875004717119518658)
XLA Ops:
  0.6 0.0 copy-start
  0.6 56.7 %exchange.1 = (f32[128,8,512]{2,1,0:T(8,128)S(1)}, f32[2,512,512]{2,1,0:T(8,128)S(1)}) custom-call(s32[128]{0:T(128)} %assign_ref.3, f32[128,8,512]{2,1,0:T(8,128)} %momentum_hbm.1, bf16[512,512]{1,0:T(8,128)(2,1)} %hidden_hbm.1, bf16[512,512]{1,0:T(8,128)(2,1)} %grads_hbm.1, s32[1,512]{1,0:T(1,128)} %bitcast.1), custom_call_target="tpu_custom_call" | custom-call | tf_op jit(solution)/shard_map/exchange/pallas_call | solution.py:328
  57.3 0.0 copy-done
  57.3 2.5 %place.1 = (f32[128,8,512]{2,1,0:T(8,128)}, f32[2,512,512]{2,1,0:T(8,128)}) custom-call(s32[128]{0:T(128)S(1)} %copy-done, f32[128,8,512]{2,1,0:T(8,128)S(1)} %get-tuple-element.4.new_ref, f32[2,512,512]{2,1,0:T(8,128)S(1)} %get-tuple-element.5.update_ref), custom_call_target="tpu_custom_call" | custom-call | tf_op jit(solution)/shard_map/place/pallas_call | solution.py:374
Async XLA Ops:
  0.6 56.7 %copy-start = (s32[128]{0:T(128)S(1)}, s32[128]{0:T(128)}, u32[]{:S(2)}) copy-start(s32[128]{0:T(128)} %assign_ref.3) | copy-start | bytes 1540

commit v5 on v4

--- a/solution.py
+++ b/solution.py
@@ -28,13 +28,15 @@
 
 
 def exchange_kernel(
-    assign_ref,
+    assign_hbm,
     momentum_hbm,
     hidden_hbm,
     grads_hbm,
-    routing_ref,
+    routing_hbm,
     new_ref,
     update_ref,
+    assign_ref,
+    routing_ref,
     mom,
     hid,
     out_grads,
@@ -78,11 +80,6 @@
         dz = nz // 2 + (i % 2) * ((i + 1) // 2) - (1 - i % 2) * (i // 2)
         return dz, w // nk, w % nk
 
-    def peer(n):
-        dz, dx, dk = offsets(n)
-        pz, px, pk = (z + dz) % nz, (x + dx) % nx, (k + dk) % nk
-        return (pz * nx + px) * nk + pk, (pz, px, pk, c)
-
     def sender(n):
         dz, dx, dk = offsets(n)
         return (((z + nz - dz) % nz) * nx + (x + nx - dx) % nx) * nk + (k + nk - dk) % nk
@@ -107,14 +104,21 @@
             barrier, inc=1, device_id=(z, x, k, lax.rem(c + d, nc)), device_id_type=MESH
         )
 
+    pairs = (
+        (assign_hbm, assign_ref),
+        (momentum_hbm, mom),
+        (hidden_hbm, hid),
+        (grads_hbm, out_grads),
+        (routing_hbm, routing_ref),
+    )
     loads = [
-        pltpu.make_async_copy(momentum_hbm, mom, load_sem.at[0]),
-        pltpu.make_async_copy(hidden_hbm, hid, load_sem.at[1]),
-        pltpu.make_async_copy(grads_hbm, out_grads, load_sem.at[2]),
+        pltpu.make_async_copy(source, target, load_sem.at[i])
+        for i, (source, target) in enumerate(pairs)
     ]
     for copy in loads:
         copy.start()
     loads[0].wait()
+    loads[1].wait()
     def convert(j):
         @pl.loop(0, owners, unroll=4)
         def _(o):
@@ -148,14 +152,36 @@
         send_planes(0, [d] if d == half else [d, nz - d])
     send_planes(0, [0], 1)
     convert(1)
-    order = [half]
-    for d in range(half - 1, 0, -1):
-        order += [nz - d, d]
-    send_planes(1, order)
-    send_planes(1, [0], 1)
-
-    loads[1].wait()
-    loads[2].wait()
+    def paced(alpha, send):
+        late = [1 - alpha * max(0.0, 1 - p / half) for p in range(nz)]
+        turn = [(p % 2) * half + p // 2 for p in range(nz)]
+        jobs = [(i, p) for i in range(nx * nk) for p in turn]
+        for i, p in sorted(jobs, key=lambda job: (job[0] + 1) * late[job[1]]):
+            w = nx * nk - 1 - i
+            px, pk = xs[w // nk], ks[w % nk]
+
+            def go(p=p, i=i, px=px, pk=pk):
+                send(i, (p * nx + px) * nk + pk, (p, px, pk, c))
+
+            if w > 0:
+                go()
+            else:
+                pl.when(z != p)(go)
+
+    def send_second(i, to, where):
+        pltpu.make_async_remote_copy(
+            src_ref=m_send.at[1, to],
+            dst_ref=m_recv.at[1, me],
+            send_sem=m_ssem.at[1],
+            recv_sem=m_rsem.at[1],
+            device_id=where,
+            device_id_type=MESH,
+        ).start()
+
+    paced(0.1, send_second)
+
+    for copy in loads[2:]:
+        copy.wait()
     hid_t = hid[...].T
     for j in range(2):
         m_recv[j, me] = m_send[j, me]
@@ -167,28 +193,30 @@
             at = pl.multiple_of(o * rows, rows)
             g_send[o, j] = upd32[j, pl.ds(at, rows), :].astype(jnp.bfloat16)
 
-    @pl.loop(0, owners - 1)
-    def _(n):
-        to, where = peer(n)
+    def send_back(i, to, where):
         pltpu.make_async_remote_copy(
             src_ref=g_send.at[to],
             dst_ref=g_recv.at[me],
             send_sem=g_ssem,
-            recv_sem=g_rsem.at[n // nz],
+            recv_sem=g_rsem.at[i],
             device_id=where,
             device_id_type=MESH,
         ).start()
 
+    paced(0.2, send_back)
+
     g_recv[me] = g_send[me]
 
-    def spread(source, target, send, recv, j):
-        for d in range(1, nc):
-            to = (c + d) % nc
+    depth = part.shape[2] // 2
+
+    def spread(source, target, send, recv, j, h):
+        for d in (2, 1, 3):
+            to = lax.rem(c + d, nc)
             pltpu.make_async_remote_copy(
                 src_ref=source(to),
                 dst_ref=target,
                 send_sem=send.at[j],
-                recv_sem=recv.at[j],
+                recv_sem=recv.at[j, h],
                 device_id=(z, x, k, to),
                 device_id_type=MESH,
             ).start()
@@ -208,46 +236,78 @@
 
         ub[j] = upd32[j].astype(jnp.bfloat16)
         product = dot_rows(ub[j], ub[j])
+        product = product.astype(jnp.bfloat16)
         for b in range(nc):
-            for t in range(3):
-                at = (b + t) % nc * blk
-                part[j, b, t] = product[b * blk : (b + 1) * blk, at : at + blk].astype(jnp.bfloat16)
-        spread(lambda to: part.at[j, to], part_recv.at[j, c], p_ssem, p_rsem, j)
+            own = product[b * blk : (b + 1) * blk]
+            after = (b + 1) % nc * blk
+            top, left = b % 2 * blk + b // 2 * (blk // 2), (b % 2 + 2) * blk
+            part[j, b, 0:blk] = own[:, b * blk : (b + 1) * blk]
+            part[j, b, blk : 2 * blk] = own[:, after : after + blk]
+            part[j, b, 2 * blk :] = product[top : top + blk // 2, left : left + blk]
+        for h in range(2):
+            piece = pl.ds(h * depth, depth)
+            spread(
+                lambda to: part.at[j, to, piece], part_recv.at[j, c, piece], p_ssem, p_rsem, j, h
+            )
         part_recv[j, c] = part[j, c]
 
     def sum_parts(j):
-        arrived(part_recv.at[j, pl.ds(0, nc - 1)], p_rsem.at[j])
-        total = part_recv[j, 0].astype(jnp.float32)
-        for b in range(1, nc):
-            total = total + part_recv[j, b].astype(jnp.float32)
-        whole_send[j] = total.astype(jnp.bfloat16)
-        spread(lambda to: whole_send.at[j], whole_recv.at[j, c], w_ssem, w_rsem, j)
+        for h in range(2):
+            piece = pl.ds(h * depth, depth)
+            arrived(part_recv.at[j, pl.ds(0, nc - 1), piece], p_rsem.at[j, h])
+            total = part_recv[j, 0, piece].astype(jnp.float32)
+            for b in range(1, nc):
+                total = total + part_recv[j, b, piece].astype(jnp.float32)
+            whole_send[j, piece] = total.astype(jnp.bfloat16)
+            spread(
+                lambda to: whole_send.at[j, piece],
+                whole_recv.at[j, c, piece],
+                w_ssem,
+                w_rsem,
+                j,
+                h,
+            )
         whole_recv[j, c] = whole_send[j]
 
     partial_gram(0)
     sum_parts(0)
     partial_gram(1)
+    sum_parts(1)
 
     @pl.loop(0, 2)
     def _(j):
-        arrived(whole_recv.at[j, pl.ds(0, nc - 1)], w_rsem.at[j])
+        for h in range(2):
+            piece = pl.ds(h * depth, depth)
+            arrived(whole_recv.at[j, pl.ds(0, nc - 1), piece], w_rsem.at[j, h])
         eye = lax.broadcasted_iota(jnp.int32, (blk, blk), 0) == lax.broadcasted_iota(
             jnp.int32, (blk, blk), 1
         )
         diagonal = jnp.zeros((blk, blk), jnp.float32)
         for b in range(nc):
-            diagonal = diagonal + jnp.where(eye, whole_recv[j, b, 0].astype(jnp.float32), 0.0)
+            diagonal = diagonal + jnp.where(
+                eye, whole_recv[j, b, 0:blk].astype(jnp.float32), 0.0
+            )
         squares = jnp.sum(
             jnp.sum(diagonal, axis=0, keepdims=True), axis=1, keepdims=True
         )
         inverse = 1.0 / (jnp.sqrt(squares) + epsilon)
+
+        def scaled(*where):
+            return (whole_recv[where].astype(jnp.float32) * inverse) * inverse
+
+        def fill(p, q, block):
+            gram[p * blk : (p + 1) * blk, q * blk : (q + 1) * blk] = block.astype(jnp.bfloat16)
+            if p != q:
+                gram[q * blk : (q + 1) * blk, p * blk : (p + 1) * blk] = block.T.astype(
+                    jnp.bfloat16
+                )
+
         for b in range(nc):
-            for t in range(3):
-                at = (b + t) % nc * blk
-                block = (whole_recv[j, b, t].astype(jnp.float32) * inverse) * inverse
-                gram[b * blk : (b + 1) * blk, at : at + blk] = block.astype(jnp.bfloat16)
-                if t == 1:
-                    gram[at : at + blk, b * blk : (b + 1) * blk] = block.T.astype(jnp.bfloat16)
+            fill(b, b, scaled(j, b, slice(0, blk)))
+            fill(b, (b + 1) % nc, scaled(j, b, slice(blk, 2 * blk)))
+            if b < 2:
+                rest = slice(2 * blk, None)
+                fill(b, b + 2, jnp.concatenate([scaled(j, b, rest), scaled(j, b + 2, rest)], 0))
         g1 = gram[...]
         p1 = (cubic_weight * g1.astype(jnp.float32) + quintic_weight * dot(g1, g1)).astype(
             jnp.bfloat16
@@ -270,10 +330,6 @@
         turned = (inverse * (linear_weight**2 * upd32[j] + dot(rest, ub[j]))).astype(jnp.bfloat16)
         update_ref[j] = scaling * turned.astype(jnp.float32)
 
-        @pl.when(j == 0)
-        def _():
-            sum_parts(1)
-
     def combine(q):
         for i in range(nz):
             o = sender(q * nz + i)
@@ -299,9 +355,14 @@
     arrived(g_send.at[pl.ds(0, owners - 1)], g_ssem)
 
 
-def place_kernel(assign_ref, new_ref, update_ref, new_hbm, out_hbm, new_sem, out_sem):
+def place_kernel(
+    assign_hbm, new_ref, update_ref, new_hbm, out_hbm, assign_ref, load_sem, new_sem, out_sem
+):
+    load = pltpu.make_async_copy(assign_hbm, assign_ref, load_sem)
+    load.start()
     copy = pltpu.make_async_copy(update_ref, out_hbm, out_sem)
     copy.start()
+    load.wait()
 
     @pl.loop(0, new_ref.shape[0], unroll=8)
     def _(s):
@@ -322,7 +383,6 @@
     scaling = 0.2 * float(max(ffe, width)) ** 0.5
     bf16, f32 = jnp.bfloat16, jnp.float32
     hbm = pl.BlockSpec(memory_space=pltpu.HBM)
-    smem = pl.BlockSpec(memory_space=pltpu.SMEM)
     vmem = pl.BlockSpec(memory_space=pltpu.VMEM)
     sem = pltpu.SemaphoreType.DMA
     placed, update = pl.pallas_call(
@@ -331,9 +391,11 @@
             pltpu.VMEM((experts, rows, cols), f32),
             pltpu.VMEM((2, ffe, cols), f32),
         ),
-        in_specs=[smem, hbm, hbm, hbm, vmem],
+        in_specs=[hbm] * 5,
         out_specs=(vmem, vmem),
         scratch_shapes=[
+            pltpu.SMEM((experts,), jnp.int32),
+            pltpu.VMEM((1, tokens), jnp.int32),
             pltpu.VMEM((experts, rows, cols), f32),
             pltpu.VMEM((tokens, ffe), bf16),
             pltpu.VMEM((tokens, cols), bf16),
@@ -343,22 +405,22 @@
             pltpu.VMEM((owners, 2, rows, cols), bf16),
             pltpu.VMEM((2, ffe, cols), f32),
             pltpu.VMEM((2, ffe, cols), bf16),
-            pltpu.VMEM((2, nc, 3, blk, blk), bf16),
-            pltpu.VMEM((2, nc, 3, blk, blk), bf16),
-            pltpu.VMEM((2, 3, blk, blk), bf16),
-            pltpu.VMEM((2, nc, 3, blk, blk), bf16),
+            pltpu.VMEM((2, nc, 5 * blk // 2, blk), bf16),
+            pltpu.VMEM((2, nc, 5 * blk // 2, blk), bf16),
+            pltpu.VMEM((2, 5 * blk // 2, blk), bf16),
+            pltpu.VMEM((2, nc, 5 * blk // 2, blk), bf16),
             pltpu.VMEM((ffe, ffe), bf16),
             pltpu.VMEM((ffe, ffe), bf16),
             pltpu.SemaphoreType.REGULAR((sizes[0] // 2 - 1,)),
-            sem((3,)),
+            sem((5,)),
             sem((2,)),
             sem((2,)),
             sem(()),
             sem((owners // sizes[0],)),
             sem((2,)),
+            sem((2, 2)),
             sem((2,)),
-            sem((2,)),
-            sem((2,)),
+            sem((2, 2)),
         ],
         compiler_params=pltpu.CompilerParams(
             collective_id=0, has_side_effects=True, vmem_limit_bytes=36 << 20
@@ -377,13 +439,13 @@
             jax.ShapeDtypeStruct((experts, rows, cols), f32),
             jax.ShapeDtypeStruct((2, ffe, cols), f32),
         ),
-        in_specs=[smem, vmem, vmem],
+        in_specs=[hbm, vmem, vmem],
         out_specs=(hbm, hbm),
-        scratch_shapes=[sem(()), sem(())],
+        scratch_shapes=[pltpu.SMEM((experts,), jnp.int32), sem(()), sem(()), sem(())],
         compiler_params=pltpu.CompilerParams(vmem_limit_bytes=4 << 20),
         name="place",
     )(
-        assignment,
+        pltpu.with_memory_space_constraint(assignment, pltpu.HBM),
         pltpu.with_memory_space_constraint(placed, pltpu.VMEM),
         pltpu.with_memory_space_constraint(update, pltpu.VMEM),
     )

time: 60 us -> 58.1 us (0.968)
  Pallas kernels: 59.2 us -> 57.4 us
    pallas_call x1, Pallas kernels: 56.7 us -> 55.4 us  [body(): pl.pallas_call(functools.partial(exchange_kernel, sizes=sizes, scaling=sc...]
where the time goes in v5:
time: 58.1 us; the launch traced here: 58 us
  Pallas kernels  57.4 us (99%)
  between operations  0.64 us (1%)
    pallas_call x1, Pallas kernels, body(): pl.pallas_call(functools.partial(exchange_kernel, sizes=sizes, scaling=sc...  55.4 us
    pallas_call x1, Pallas kernels, body(): pl.pallas_call(place_kernel, out_shape=(jax.ShapeDtypeStruct((experts, ro...  1.99 us

profile of v5, /device:TPU:8, one launch (start us, length us, event | category | flops | bytes accessed | tf_op | source)
XLA Modules:
  0.0 58.0 jit_solution(13865027708614888311)
XLA Ops:
  0.6 55.4 %exchange.1 = (f32[128,8,512]{2,1,0:T(8,128)S(1)}, f32[2,512,512]{2,1,0:T(8,128)S(1)}) custom-call(s32[128]{0:T(128)} %assign_hbm.3, f32[128,8,512]{2,1,0:T(8,128)} %momentum_hbm.1, bf16[512,512]{1,0:T(8,128)(2,1)} %hidden_hbm.1, bf16[512,512]{1,0:T(8,128)(2,1)} %grads_hbm.1, s32[1,512]{1,0:T(1,128)} %bitcast.1), custom_call_target="tpu_custom_call" | custom-call | tf_op jit(solution)/shard_map/exchange/pallas_call | solution.py:388
  56.0 2.0 %place.1 = (f32[128,8,512]{2,1,0:T(8,128)}, f32[2,512,512]{2,1,0:T(8,128)}) custom-call(s32[128]{0:T(128)} %assign_hbm.3, f32[128,8,512]{2,1,0:T(8,128)S(1)} %get-tuple-element.4.new_ref, f32[2,512,512]{2,1,0:T(8,128)S(1)} %get-tuple-element.5.update_ref), custom_call_target="tpu_custom_call" | custom-call | tf_op jit(solution)/shard_map/place/pallas_call | solution.py:436

commit v6 on v5

--- a/solution.py
+++ b/solution.py
@@ -178,7 +178,7 @@
             device_id_type=MESH,
         ).start()
 
-    paced(0.1, send_second)
+    paced(0.05, send_second)
 
     for copy in loads[2:]:
         copy.wait()
@@ -203,7 +203,7 @@
             device_id_type=MESH,
         ).start()
 
-    paced(0.2, send_back)
+    paced(0.15, send_back)
 
     g_recv[me] = g_send[me]
 
@@ -327,8 +327,7 @@
         rest = (
             linear_weight * (p1.astype(jnp.float32) + p2.astype(jnp.float32)) + dot(p2, p1)
         ).astype(jnp.bfloat16)
-        turned = (inverse * (linear_weight**2 * upd32[j] + dot(rest, ub[j]))).astype(jnp.bfloat16)
-        update_ref[j] = scaling * turned.astype(jnp.float32)
+        update_ref[j] = (scaling * inverse) * (linear_weight**2 * upd32[j] + dot(rest, ub[j]))
 
     def combine(q):
         for i in range(nz):

time: 58.1 us -> 58.1 us (level)
  no operation moved by 1% of the time
where the time goes in v6:
time: 58.1 us; the launch traced here: 58 us
  Pallas kernels  57.3 us (99%)
  between operations  0.64 us (1%)
    pallas_call x1, Pallas kernels, body(): pl.pallas_call(functools.partial(exchange_kernel, sizes=sizes, scaling=sc...  55.3 us
    pallas_call x1, Pallas kernels, body(): pl.pallas_call(place_kernel, out_shape=(jax.ShapeDtypeStruct((experts, ro...  1.99 us

profile of v6, /device:TPU:8, one launch (start us, length us, event | category | flops | bytes accessed | tf_op | source)
XLA Modules:
  0.0 58.0 jit_solution(9764925111549154497)
XLA Ops:
  0.6 55.3 %exchange.1 = (f32[128,8,512]{2,1,0:T(8,128)S(1)}, f32[2,512,512]{2,1,0:T(8,128)S(1)}) custom-call(s32[128]{0:T(128)} %assign_hbm.3, f32[128,8,512]{2,1,0:T(8,128)} %momentum_hbm.1, bf16[512,512]{1,0:T(8,128)(2,1)} %hidden_hbm.1, bf16[512,512]{1,0:T(8,128)(2,1)} %grads_hbm.1, s32[1,512]{1,0:T(1,128)} %bitcast.1), custom_call_target="tpu_custom_call" | custom-call | tf_op jit(solution)/shard_map/exchange/pallas_call | solution.py:387
  56.0 2.0 %place.1 = (f32[128,8,512]{2,1,0:T(8,128)}, f32[2,512,512]{2,1,0:T(8,128)}) custom-call(s32[128]{0:T(128)} %assign_hbm.3, f32[128,8,512]{2,1,0:T(8,128)S(1)} %get-tuple-element.4.new_ref, f32[2,512,512]{2,1,0:T(8,128)S(1)} %get-tuple-element.5.update_ref), custom_call_target="tpu_custom_call" | custom-call | tf_op jit(solution)/shard_map/place/pallas_call | solution.py:435

commit v7 on v6

--- a/solution.py
+++ b/solution.py
@@ -84,6 +84,19 @@
         dz, dx, dk = offsets(n)
         return (((z + nz - dz) % nz) * nx + (x + nx - dx) % nx) * nk + (k + nk - dk) % nk
 
+    pairs = (
+        (assign_hbm, assign_ref),
+        (momentum_hbm, mom),
+        (hidden_hbm, hid),
+        (grads_hbm, out_grads),
+        (routing_hbm, routing_ref),
+    )
+    loads = [
+        pltpu.make_async_copy(source, target, load_sem.at[i])
+        for i, (source, target) in enumerate(pairs)
+    ]
+    for copy in loads[:2]:
+        copy.start()
     zs = [lax.rem(z + d, nz) for d in range(nz)]
     xs = [lax.rem(x + d, nx) for d in range(nx)]
     ks = [lax.rem(k + d, nk) for d in range(nk)]
@@ -104,19 +117,6 @@
             barrier, inc=1, device_id=(z, x, k, lax.rem(c + d, nc)), device_id_type=MESH
         )
 
-    pairs = (
-        (assign_hbm, assign_ref),
-        (momentum_hbm, mom),
-        (hidden_hbm, hid),
-        (grads_hbm, out_grads),
-        (routing_hbm, routing_ref),
-    )
-    loads = [
-        pltpu.make_async_copy(source, target, load_sem.at[i])
-        for i, (source, target) in enumerate(pairs)
-    ]
-    for copy in loads:
-        copy.start()
     loads[0].wait()
     loads[1].wait()
     def convert(j):
@@ -139,6 +139,8 @@
                 ).start()
 
     convert(0)
+    for copy in loads[2:]:
+        copy.start()
     pl.semaphore_wait(barrier, 3 * nx * nk - 1 + nc - 1)
     half = nz // 2
     for d in range(1, half + 1):

time: 58.1 us -> 58.1 us (level)
  no operation moved by 1% of the time
where the time goes in v7:
time: 58.1 us; the launch traced here: 58 us
  Pallas kernels  57.3 us (99%)
  between operations  0.64 us (1%)
    pallas_call x1, Pallas kernels, body(): pl.pallas_call(functools.partial(exchange_kernel, sizes=sizes, scaling=sc...  55.3 us
    pallas_call x1, Pallas kernels, body(): pl.pallas_call(place_kernel, out_shape=(jax.ShapeDtypeStruct((experts, ro...  1.99 us

profile of v7, /device:TPU:8, one launch (start us, length us, event | category | flops | bytes accessed | tf_op | source)
XLA Modules:
  0.0 58.0 jit_solution(15293082063342379622)
XLA Ops:
  0.6 55.3 %exchange.1 = (f32[128,8,512]{2,1,0:T(8,128)S(1)}, f32[2,512,512]{2,1,0:T(8,128)S(1)}) custom-call(s32[128]{0:T(128)} %assign_hbm.3, f32[128,8,512]{2,1,0:T(8,128)} %momentum_hbm.1, bf16[512,512]{1,0:T(8,128)(2,1)} %hidden_hbm.1, bf16[512,512]{1,0:T(8,128)(2,1)} %grads_hbm.1, s32[1,512]{1,0:T(1,128)} %bitcast.1), custom_call_target="tpu_custom_call" | custom-call | tf_op jit(solution)/shard_map/exchange/pallas_call | solution.py:389
  56.0 2.0 %place.1 = (f32[128,8,512]{2,1,0:T(8,128)}, f32[2,512,512]{2,1,0:T(8,128)}) custom-call(s32[128]{0:T(128)} %assign_hbm.3, f32[128,8,512]{2,1,0:T(8,128)S(1)} %get-tuple-element.4.new_ref, f32[2,512,512]{2,1,0:T(8,128)S(1)} %get-tuple-element.5.update_ref), custom_call_target="tpu_custom_call" | custom-call | tf_op jit(solution)/shard_map/place/pallas_call | solution.py:437
